TPU v7x, 128 devices: a whole 4x4x4 slice. The times are simulated.
128 devices in a mesh: ctx: 32 (over x, y, core), head: 4 (over z).
Axes of the slice: x: 4, y: 4, z: 4, core: 2. Of those that a mesh axis runs over, the one named last changes fastest.
Arguments:
- tokens: bfloat16 [8192, 2048], P(('ctx', 'head')), may hold values from -6 to 6
- w_query: bfloat16 [2048, 2048], P(None, 'head'), may hold values from -0.125 to 0.125
- w_key_first: bfloat16 [2048, 2048], P(None, 'head'), may hold values from -0.125 to 0.125
- w_key_second: bfloat16 [2048, 2048], P(None, 'head'), may hold values from -0.125 to 0.125
- w_value_first: bfloat16 [2048, 2048], P(None, 'head'), may hold values from -0.125 to 0.125
- w_value_second: bfloat16 [2048, 2048], P(None, 'head'), may hold values from -0.125 to 0.125
- w_out: bfloat16 [2048, 2048], P('head'), may hold values from -0.125 to 0.125
- lengths: int32 [16], replicated, may hold values from 1 to 4352, 8192 in all
- out_cotangent: bfloat16 [8192, 2048], P(('ctx', 'head')), may hold values from -6 to 6
Outputs:
- result: bfloat16 [8192, 2048], P(('ctx', 'head'))
- grad_tokens: bfloat16 [8192, 2048], P(('ctx', 'head'))
Inputs may be any that keep to these rules, and one draw needn't show every extreme that they name: Document lengths sum to 8192; the longest holds exactly 4352 tokens.
All inputs are finite; a program needn't handle non-finite values.
Results may differ from a plain program's by a relative error of at most 0.012.
Values may be sent and summed in bfloat16 or wider, within the bound.
No kernel may reach another device: no remote copies, remote signals or barrier semaphores. Data moves between devices by JAX's collectives and lax.ppermute only.
A program may use at most 128 MiB of HBM per device.

v0:
```python
import jax
import jax.numpy as jnp
from jax import lax
from jax.sharding import Mesh
from jax.sharding import PartitionSpec as P

HEAD_DIM = 128
GROUP = 64
CTX = ("ctx_0", "ctx_1", "ctx_2")
CTX_HEAD = ("ctx_0", "ctx_1", "ctx_2", "head")


epsilon = 1e-06
precise = lax.Precision.HIGHEST


def side_by_side(arrays, axis, dim, along):
    both = jnp.concatenate(arrays, axis=along)
    filled, at, done = (lax.all_gather(both, axis, axis=dim, tiled=True), 0, [])
    for a in arrays:
        done.append(lax.slice_in_dim(filled, at, at + a.shape[along], axis=along))
        at += a.shape[along]
    return tuple(done)


def filled_with(value, identity):
    return jax.tree.map(
        lambda a, e: jnp.broadcast_to(jnp.asarray(e, a.dtype), a.shape), value, identity
    )


def carried_in(value, axes, combine, identity, reverse):
    before = start = filled_with(value, identity)
    so_far = value
    for axis in reversed(axes):
        count, here = (lax.axis_size(axis), lax.axis_index(axis))
        pieces = jax.tree.map(lambda part: lax.all_gather(part, axis), so_far)
        inside, so_far = (start, start)
        for k in reversed(range(count)) if reverse else range(count):
            passed = k > here if reverse else k < here
            so_far = combine(so_far, jax.tree.map(lambda part: part[k], pieces))
            inside = jax.tree.map(lambda new, old: jnp.where(passed, new, old), so_far, inside)
        before = combine(inside, before)
    return before


def in_blocks(value, dim, count):
    dims = value.shape
    pieces = value.reshape(*dims[:dim], count, dims[dim] // count, *dims[dim + 1 :])
    return jnp.moveaxis(pieces, dim, 0)


def sum_at_owner(value, axis, dim):
    pieces = in_blocks(value, dim, lax.axis_size(axis))
    arrived = lax.all_to_all(pieces, axis, split_axis=0, concat_axis=0, tiled=True)
    return arrived.astype(jnp.float32).sum(axis=0)


def start_flags(lengths, positions):
    doc_first = jnp.cumsum(lengths) - lengths
    return jnp.any(positions[:, None] == doc_first[None, :], axis=1).astype(jnp.int32)


def unit_norm(raw_key):
    return raw_key / jnp.sqrt(jnp.sum(raw_key * raw_key, axis=-1, keepdims=True) + epsilon)


def group_step(memory, inputs):
    queries, key_first, key_second, value_first, value_second, starts = inputs
    block_len = queries.shape[0]
    key_rows = jnp.stack([unit_norm(key_first), unit_norm(key_second)], axis=1).reshape(
        2 * block_len, queries.shape[1], queries.shape[2]
    )
    value_rows = jnp.stack([value_first, value_second], axis=1).reshape(
        2 * block_len, value_first.shape[1], value_first.shape[2]
    )
    counts = jnp.cumsum(starts)
    counts_ref = jnp.repeat(counts, 2)
    incoming = (counts == 0).astype(jnp.float32)
    incoming_ref = (counts_ref == 0).astype(jnp.float32)
    refl_pos = jnp.arange(2 * block_len)
    token_pos = jnp.arange(block_len)
    same_doc = counts_ref[:, None] == counts_ref[None, :]
    strict_lower = jnp.logical_and(refl_pos[None, :] < refl_pos[:, None], same_doc).astype(
        jnp.float32
    )
    key_gram = jnp.einsum("rhd,shd->hrs", key_rows, key_rows, precision=precise)
    system = 2.0 * key_gram * strict_lower[None] + jnp.eye(2 * block_len, dtype=jnp.float32)[None]
    carried = jnp.einsum("rhd,hdw->hrw", key_rows, memory, precision=precise)
    right_side = 2.0 * (
        jnp.transpose(value_rows, (1, 0, 2)) - incoming_ref[None, :, None] * carried
    )
    updates = lax.linalg.triangular_solve(
        system, right_side, left_side=True, lower=True, unit_diagonal=True
    )
    visible = jnp.logical_and(
        refl_pos[None, :] <= 2 * token_pos[:, None] + 1, counts[:, None] == counts_ref[None, :]
    ).astype(jnp.float32)
    scores = jnp.einsum("thd,shd->hts", queries, key_rows, precision=precise) * visible[None]
    outputs = jnp.einsum("hts,hsw->thw", scores, updates, precision=precise)
    outputs = outputs + incoming[:, None, None] * jnp.einsum(
        "thd,hdw->thw", queries, memory, precision=precise
    )
    last_count = counts[block_len - 1]
    tail_mask = (counts_ref == last_count).astype(jnp.float32)
    keep_state = (last_count == 0).astype(jnp.float32)
    new_memory = keep_state * memory + jnp.einsum(
        "rhd,hrw->hdw", key_rows * tail_mask[:, None, None], updates, precision=precise
    )
    return (new_memory, outputs)


def recurrence(
    queries, key_first, key_second, value_first, value_second, starts, memory, block_len
):
    total_rows = queries.shape[0]
    blocks = total_rows // block_len

    def blockify(array_in):
        return array_in.reshape((blocks, block_len) + array_in.shape[1:])

    stacked = (
        blockify(queries),
        blockify(key_first),
        blockify(key_second),
        blockify(value_first),
        blockify(value_second),
        blockify(starts),
    )
    memory_end, outputs = lax.scan(jax.checkpoint(group_step), memory, stacked)
    return (outputs.reshape((total_rows,) + outputs.shape[2:]), memory_end)


def compose(earlier, later):
    joined = jnp.einsum("hij,hjk->hik", later[0], earlier[0], precision=precise)
    shifted = jnp.einsum("hij,hjk->hik", later[0], earlier[1], precision=precise) + later[1]
    return (joined, shifted)


def per_device(
    tokens,
    w_query,
    w_key_first,
    w_key_second,
    w_value_first,
    w_value_second,
    w_out,
    lengths,
    out_cotangent,
):
    weights = (w_query, w_key_first, w_key_second, w_value_first, w_value_second)
    token_rows, cotangent_rows = side_by_side((tokens, out_cotangent), "head", 0, 1)
    block_rows = token_rows.shape[0]
    local_width = w_query.shape[1]
    head_count = local_width // HEAD_DIM
    positions = lax.axis_index(CTX) * block_rows + jnp.arange(block_rows, dtype=jnp.int32)
    starts = start_flags(lengths, positions)
    projected = tuple(
        (
            jnp.dot(token_rows, weight, preferred_element_type=jnp.float32).reshape(
                block_rows, head_count, HEAD_DIM
            )
            for weight in weights
        )
    )
    zero_values = jnp.zeros((block_rows, head_count, HEAD_DIM), jnp.float32)
    value_first_ext = jnp.concatenate([projected[3], zero_values], axis=2)
    value_second_ext = jnp.concatenate([projected[4], zero_values], axis=2)
    eye_block = jnp.broadcast_to(
        jnp.eye(HEAD_DIM, dtype=jnp.float32), (head_count, HEAD_DIM, HEAD_DIM)
    )
    zero_state = jnp.zeros((head_count, HEAD_DIM, HEAD_DIM), jnp.float32)
    start_ext = jnp.concatenate([zero_state, eye_block], axis=2)
    outputs_ext, memory_ext = recurrence(
        projected[0],
        projected[1],
        projected[2],
        value_first_ext,
        value_second_ext,
        starts,
        start_ext,
        GROUP,
    )
    local_out = outputs_ext[:, :, :HEAD_DIM]
    reach_rows = outputs_ext[:, :, HEAD_DIM:]
    offset = memory_ext[:, :, :HEAD_DIM]
    transition = memory_ext[:, :, HEAD_DIM:]
    identity = (eye_block, zero_state)
    start_memory = carried_in((transition, offset), CTX, compose, identity, False)[1]
    mixed = local_out + jnp.einsum("thd,hdw->thw", reach_rows, start_memory, precision=precise)
    inv_rms = lax.rsqrt(jnp.mean(mixed * mixed, axis=-1, keepdims=True) + epsilon)
    normal = mixed * inv_rms
    normed = normal.astype(jnp.bfloat16).reshape(block_rows, local_width)
    share_rows = block_rows // lax.axis_size("head")
    row_block = normed
    result = sum_at_owner(
        jnp.dot(row_block, w_out, preferred_element_type=jnp.float32).astype(jnp.bfloat16),
        "head",
        0,
    ).astype(jnp.bfloat16)
    grad_normed = lax.dot_general(
        cotangent_rows, w_out, (((1,), (1,)), ((), ())), preferred_element_type=jnp.float32
    ).reshape(block_rows, head_count, HEAD_DIM)
    grad_mixed = inv_rms * (
        grad_normed - normal * jnp.mean(grad_normed * normal, axis=-1, keepdims=True)
    )
    carried = jnp.einsum("thd,thw->hdw", reach_rows, grad_mixed, precision=precise)
    back_trans = jnp.swapaxes(transition, 1, 2)
    end_grad = carried_in((back_trans, carried), CTX, compose, identity, True)[1]

    def mixer_local(queries, key_first, key_second, value_first, value_second):
        return recurrence(
            queries, key_first, key_second, value_first, value_second, starts, start_memory, GROUP
        )

    recomputed, pullback = jax.vjp(
        mixer_local, projected[0], projected[1], projected[2], projected[3], projected[4]
    )
    proj_grads = pullback((grad_mixed, end_grad))
    rounded = tuple(
        (
            grad_part.reshape(block_rows, local_width).astype(jnp.bfloat16)
            for grad_part in proj_grads
        )
    )
    summed = jnp.zeros((share_rows * lax.axis_size("head"), w_query.shape[0]), jnp.float32)
    for grad_part, weight in zip(rounded, weights):
        row_block = grad_part
        summed = summed + lax.dot_general(
            row_block, weight, (((1,), (1,)), ((), ())), preferred_element_type=jnp.float32
        )
    grad_tokens = sum_at_owner(summed.astype(jnp.bfloat16), "head", 0).astype(jnp.bfloat16)
    return (result, grad_tokens)


def solution(mesh):
    finer = Mesh(
        mesh.devices.reshape(4, 4, 2, mesh.shape["head"]), ("ctx_0", "ctx_1", "ctx_2", "head")
    )
    placed = (
        P(CTX_HEAD, None),
        P(None, "head"),
        P(None, "head"),
        P(None, "head"),
        P(None, "head"),
        P(None, "head"),
        P("head", None),
        P(),
        P(CTX_HEAD, None),
    )
    return jax.shard_map(
        per_device,
        mesh=finer,
        in_specs=placed,
        out_specs=(P(CTX_HEAD, None), P(CTX_HEAD, None)),
        check_vma=False,
    )
```

profile of v0, /device:TPU:0, one launch (start us, length us, event | category | flops | bytes accessed | tf_op | source)
XLA Modules:
  0.0 949.9 jit_solution(18445076470511364727)
XLA Ops:
  11.1 32.1 %all-gather.22.cloned.1.call-done = bf16[256,4096]{1,0:T(8,128)(2,1)} async-done(((bf16[64,4096]{1,0:T(8,128)(2,1)}), bf16[256,4096]{1,0:T(8,128)(2,1)}) %all-gather.22.cloned.1.call-update) | async-done | bytes 2097168 | tf_op jit(solution)/shard_map/all_gather | solution.py:19
  67.4 232.6 %while.49 = (s32[]{:T(128)}, f32[4,128,256]{2,1,0:T(8,128)S(1)}, f32[4,64,4,256]{3,1,0,2:T(8,128)}, s32[4,64]{1,0:T(4,128)S(1)}, f32[4,64,4,128]{3,1,2,0:T(8,128...) while((s32[]{:T(128)}, f32[4,128,256]{2,1,0:T(8,128)S(1)}, ...), condition=%wide.region_6.7_spmd, body=%wide.region_2.6_spmd.sunk | while | flops 958026560 | bytes 15452111 | solution.py:130
  79.6 39.9 %custom-call.20 = f32[4,1,128,128]{2,3,1,0:T(8,128)} custom-call(f32[4,1,128,128]{3,2,1,0:T(8,128)S(1)} %fusion.459), custom_call_target="InvertDiagBlocksLowerTriangular" | custom-call | tf_op jit(solution)/shard_map/while/body/eval_jaxpr/checkpoint/triangular_solve | solution.py:93
  137.8 39.9 %custom-call.20 = f32[4,1,128,128]{2,3,1,0:T(8,128)} custom-call(f32[4,1,128,128]{3,2,1,0:T(8,128)S(1)} %fusion.459), custom_call_target="InvertDiagBlocksLowerTriangular" | custom-call | tf_op jit(solution)/shard_map/while/body/eval_jaxpr/checkpoint/triangular_solve | solution.py:93
  196.0 39.9 %custom-call.20 = f32[4,1,128,128]{2,3,1,0:T(8,128)} custom-call(f32[4,1,128,128]{3,2,1,0:T(8,128)S(1)} %fusion.459), custom_call_target="InvertDiagBlocksLowerTriangular" | custom-call | tf_op jit(solution)/shard_map/while/body/eval_jaxpr/checkpoint/triangular_solve | solution.py:93
  254.1 39.9 %custom-call.20 = f32[4,1,128,128]{2,3,1,0:T(8,128)} custom-call(f32[4,1,128,128]{3,2,1,0:T(8,128)S(1)} %fusion.459), custom_call_target="InvertDiagBlocksLowerTriangular" | custom-call | tf_op jit(solution)/shard_map/while/body/eval_jaxpr/checkpoint/triangular_solve | solution.py:93
  308.8 20.0 %all-gather.24.cloned.1.call-done = f32[16,128,128]{2,1,0:T(8,128)} async-done(((f32[4,128,128]{2,1,0:T(8,128)}), f32[16,128,128]{2,1,0:T(8,128)}) %all-gather.24.cloned.1.call-update) | async-done | bytes 1048592 | tf_op jit(solution)/shard_map/all_gather | solution.py:37
  334.6 20.2 %all-gather.28.cloned.1.call-done = f32[16,128,128]{2,1,0:T(8,128)} async-done(((f32[4,128,128]{2,1,0:T(8,128)}), f32[16,128,128]{2,1,0:T(8,128)}) %all-gather.28.cloned.1.call-update) | async-done | bytes 1048592 | tf_op jit(solution)/shard_map/all_gather | solution.py:37
  374.5 6.7 all-gather.26.cloned.1.call-done
  381.2 25.8 %all-gather.30.cloned.1.call-done = f32[16,128,128]{2,1,0:T(8,128)} async-done(((f32[4,128,128]{2,1,0:T(8,128)}), f32[16,128,128]{2,1,0:T(8,128)}) %all-gather.30.cloned.1.call-update) | async-done | bytes 1048592 | tf_op jit(solution)/shard_map/all_gather | solution.py:37
  416.1 12.1 %all-gather.9 = f32[8,128,128]{2,1,0:T(8,128)S(1)} all-gather(f32[4,128,128]{2,1,0:T(8,128)S(1)} %fusion.109), channel_id=11, replica_groups=mesh['ctx_0'=4,'ctx_1'=4,'ctx_2'=2,'head'=4] {'ctx_2'}, dimensions={0}, use_global_device_ids=true | all-gather | bytes 786432 | tf_op jit(solution)/shard_map/all_gather | solution.py:37
  451.0 4.4 all-to-all-start
  463.2 193.6 %while.51 = (s32[]{:T(128)}, f32[4,128,128]{2,1,0:T(8,128)S(1)}, f32[4,4,128,128]{3,2,1,0:T(8,128)}, s32[4,64]{1,0:T(4,128)S(1)}, f32[4,64,4,128]{3,1,2,0:T(8,12...) while((s32[]{:T(128)}, f32[4,128,128]{2,1,0:T(8,128)S(1)}, ...), condition=%wide.region_14.16_spmd.clone, body=%wide.region_10.15_spmd.clone.sunk | while | flops 403788352 | bytes 6995875 | solution.py:130
  470.3 39.3 %custom-call.22 = f32[4,1,128,128]{2,3,1,0:T(8,128)S(1)} custom-call(f32[4,1,128,128]{3,2,1,0:T(8,128)S(1)} %fusion.532), custom_call_target="InvertDiagBlocksLowerTriangular" | custom-call | tf_op jit(solution)/shard_map/jvp()/while/body/eval_jaxpr/triangular_solve/custom-call.0 | solution.py:93
  518.7 39.3 %custom-call.22 = f32[4,1,128,128]{2,3,1,0:T(8,128)S(1)} custom-call(f32[4,1,128,128]{3,2,1,0:T(8,128)S(1)} %fusion.532), custom_call_target="InvertDiagBlocksLowerTriangular" | custom-call | tf_op jit(solution)/shard_map/jvp()/while/body/eval_jaxpr/triangular_solve/custom-call.0 | solution.py:93
  567.1 39.3 %custom-call.22 = f32[4,1,128,128]{2,3,1,0:T(8,128)S(1)} custom-call(f32[4,1,128,128]{3,2,1,0:T(8,128)S(1)} %fusion.532), custom_call_target="InvertDiagBlocksLowerTriangular" | custom-call | tf_op jit(solution)/shard_map/jvp()/while/body/eval_jaxpr/triangular_solve/custom-call.0 | solution.py:93
  615.5 39.3 %custom-call.22 = f32[4,1,128,128]{2,3,1,0:T(8,128)S(1)} custom-call(f32[4,1,128,128]{3,2,1,0:T(8,128)S(1)} %fusion.532), custom_call_target="InvertDiagBlocksLowerTriangular" | custom-call | tf_op jit(solution)/shard_map/jvp()/while/body/eval_jaxpr/triangular_solve/custom-call.0 | solution.py:93
  663.7 249.7 %while.50 = (s32[]{:T(128)}, f32[4,128,128]{2,1,0:T(8,128)S(1)}, bf16[4,64,4,128]{3,1,2,0:T(8,128)(2,1)S(1)}, bf16[4,64,4,128]{3,1,2,0:T(8,128)(2,1)S(1)}, bf16[...) while((s32[]{:T(128)}, f32[4,128,128]{2,1,0:T(8,128)S(1)}, ...), condition=%wide.region_21.24_spmd, body=%wide.region_15.23_spmd.sunk | while | flops 1563188480 | bytes 27320700 | solution.py:130
  674.4 39.3 %custom-call.21 = f32[4,1,128,128]{2,3,1,0:T(8,128)S(1)} custom-call(f32[4,1,128,128]{3,2,1,0:T(8,128)S(1)} %fusion.506), custom_call_target="InvertDiagBlocksLowerTriangular" | custom-call | tf_op jit(solution)/shard_map/transpose(jvp())/while/body/eval_jaxpr/checkpoint/triangular_solve/custom-call.2 | solution.py:93
  736.7 39.3 %custom-call.21 = f32[4,1,128,128]{2,3,1,0:T(8,128)S(1)} custom-call(f32[4,1,128,128]{3,2,1,0:T(8,128)S(1)} %fusion.506), custom_call_target="InvertDiagBlocksLowerTriangular" | custom-call | tf_op jit(solution)/shard_map/transpose(jvp())/while/body/eval_jaxpr/checkpoint/triangular_solve/custom-call.2 | solution.py:93
  799.1 39.3 %custom-call.21 = f32[4,1,128,128]{2,3,1,0:T(8,128)S(1)} custom-call(f32[4,1,128,128]{3,2,1,0:T(8,128)S(1)} %fusion.506), custom_call_target="InvertDiagBlocksLowerTriangular" | custom-call | tf_op jit(solution)/shard_map/transpose(jvp())/while/body/eval_jaxpr/checkpoint/triangular_solve/custom-call.2 | solution.py:93
  861.4 39.3 %custom-call.21 = f32[4,1,128,128]{2,3,1,0:T(8,128)S(1)} custom-call(f32[4,1,128,128]{3,2,1,0:T(8,128)S(1)} %fusion.506), custom_call_target="InvertDiagBlocksLowerTriangular" | custom-call | tf_op jit(solution)/shard_map/transpose(jvp())/while/body/eval_jaxpr/checkpoint/triangular_solve/custom-call.2 | solution.py:93
  923.3 4.5 all-to-all-start.1
  929.9 12.0 %all-to-all-done.1 = bf16[4,64,2048]{2,1,0:T(8,128)(2,1)S(1)} async-done(((bf16[4,64,2048]{2,1,0:T(8,128)(2,1)}), bf16[4,64,2048]{2,1,0:T(8,128)(2,1)S(1)}, u32[]{:S(2)}, u32[]{:S(2)}) %all-to-all-start.1) | async-done | bytes 1048608 | tf_op jit(solution)/shard_map/all_to_all | solution.py:55
  (746 shorter events, 311.8 us)
Async XLA Ops:
  7.2 353.2 %copy-start = (bf16[512,2048]{1,0:T(8,128)(2,1)S(1)}, bf16[512,2048]{1,0:T(8,128)(2,1)}, u32[]{:S(2)}) copy-start(bf16[512,2048]{1,0:T(8,128)(2,1)} %param.25) | copy-start | bytes 6291460
  7.2 36.1 %all-gather.22.cloned.1.call-start = ((), (), s32[]{:S(2)}) async-start(), calls=%async_computation.2 | async-start | bytes 2621440 | tf_op jit(solution)/shard_map/all_gather | solution.py:19
  9.3 319.6 %all-gather.24.cloned.1.call-start = ((), (), s32[]{:S(2)}) async-start(), calls=%async_computation.3 | async-start | bytes 1310720 | tf_op jit(solution)/shard_map/all_gather | solution.py:37
  59.7 5.5 copy-start.39
  304.8 50.0 %all-gather.28.cloned.1.call-start = ((), (), s32[]{:S(2)}) async-start(), calls=%async_computation.5 | async-start | bytes 1310720 | tf_op jit(solution)/shard_map/all_gather | solution.py:37
  308.8 72.4 %all-gather.26.cloned.1.call-start = ((), (), s32[]{:S(2)}) async-start(), calls=%async_computation.4 | async-start | bytes 1310720 | tf_op jit(solution)/shard_map/all_gather | solution.py:37
  332.3 25.4 %copy-start.9 = (f32[4,128,128]{2,1,0:T(8,128)}, f32[4,128,128]{2,1,0:T(8,128)S(1)}, u32[]{:S(2)}) copy-start(f32[4,128,128]{2,1,0:T(8,128)S(1)} %fusion.218) | copy-start | bytes 786436
  334.6 72.4 %all-gather.30.cloned.1.call-start = ((), (), s32[]{:S(2)}) async-start(), calls=%async_computation.6 | async-start | bytes 1310720 | tf_op jit(solution)/shard_map/all_gather | solution.py:37
  360.2 77.5 %all-gather.32.cloned.1.call-start = ((), (), s32[]{:S(2)}) async-start(), calls=%async_computation.7 | async-start | bytes 1310720 | tf_op jit(solution)/shard_map/all_gather | solution.py:37
  360.3 4.1 copy-start.43
  364.4 48.1 %copy-start.8 = (f32[256,4,128]{2,0,1:T(8,128)}, f32[256,4,128]{2,0,1:T(8,128)S(1)}, u32[]{:S(2)}) copy-start(f32[256,4,128]{2,0,1:T(8,128)S(1)} %copy.179) | copy-start | bytes 1572868
  364.4 5.9 copy-start.10
  370.3 88.6 %all-gather.36.cloned.1.call-start = ((), (), s32[]{:S(2)}) async-start(), calls=%async_computation.9 | async-start | bytes 1310720 | tf_op jit(solution)/shard_map/all_gather | solution.py:37
  415.0 15.4 %copy-start.7 = (f32[256,4,128]{2,0,1:T(8,128)}, f32[256,4,128]{2,0,1:T(8,128)S(1)}, u32[]{:S(2)}) copy-start(f32[256,4,128]{2,0,1:T(8,128)S(1)} %get-tuple-element.667) | copy-start | bytes 1572868
  430.5 226.8 %all-gather.34.cloned.1.call-start = ((), (), s32[]{:S(2)}) async-start(), calls=%async_computation.8 | async-start | bytes 1310720 | tf_op jit(solution)/shard_map/all_gather | solution.py:37
  430.6 6.1 copy-start.26
  430.6 6.1 copy-start.27
  437.7 4.2 copy-start.2
  451.0 472.3 %all-to-all-start = ((bf16[4,64,2048]{2,1,0:T(8,128)(2,1)}), bf16[4,64,2048]{2,1,0:T(8,128)(2,1)}, u32[]{:S(2)}, u32[]{:S(2)}) async-start(bf16[4,64,2048]{2,1,0:T(8,128)(2,1)} %bitcast.593), calls=%async_computation | async-start | bytes 2097152 | tf_op jit(solution)/shard_map/all_to_all | solution.py:55
  455.4 201.9 %all-gather.38.cloned.1.call-start = ((), (), s32[]{:S(2)}) async-start(), calls=%async_computation.10 | async-start | bytes 1310720 | tf_op jit(solution)/shard_map/all_gather | solution.py:37
  463.2 193.6 %copy-start.20 = (f32[4,128,128]{2,1,0:T(8,128)S(1)}, f32[4,128,128]{2,1,0:T(8,128)}, u32[]{:S(2)}) copy-start(f32[4,128,128]{2,1,0:T(8,128)} %fusion.135) | copy-start | bytes 786436
  463.2 193.6 %copy-start.24 = (f32[4,128,128]{2,1,0:T(8,128)S(1)}, f32[4,128,128]{2,1,0:T(8,128)}, u32[]{:S(2)}) copy-start(f32[4,128,128]{2,1,0:T(8,128)} %convolution_add_fusion.19) | copy-start | bytes 786436
  923.3 19.6 %copy-start.1 = (bf16[512,2048]{1,0:T(8,128)(2,1)S(1)}, bf16[512,2048]{1,0:T(8,128)(2,1)}, u32[]{:S(2)}) copy-start(bf16[512,2048]{1,0:T(8,128)(2,1)} %param.25) | copy-start | bytes 6291460
  923.3 18.7 %all-to-all-start.1 = ((bf16[4,64,2048]{2,1,0:T(8,128)(2,1)}), bf16[4,64,2048]{2,1,0:T(8,128)(2,1)S(1)}, u32[]{:S(2)}, u32[]{:S(2)}) async-start(bf16[4,64,2048]{2,1,0:T(8,128)(2,1)} %bitcast.594), calls=%async_computation.1 | async-start | bytes 2097152 | tf_op jit(solution)/shard_map/all_to_all | solution.py:55
  (59 other events, 99.7 us)
Sparse Core Ops, SparseCore 0:
  9.7 33.5 all-gather.21
  304.9 23.8 all-gather.23
  330.5 24.2 all-gather.27
  356.9 24.2 all-gather.25
  382.7 24.2 all-gather.29
  408.5 24.3 all-gather.31
  434.5 24.2 all-gather.35
  460.5 24.6 all-gather.33
  487.5 24.3 all-gather.37
where the time goes:
time: 961 us; the launch traced here: 950 us
  other arithmetic  521 us (54%)
  matrix products  160 us (17%)
  waiting for transfers between devices  120 us (12%)
  local copies, waits for them, and re-layouts  93.8 us (10%)
  blocking collectives  19.3 us (2%)
  between operations  15.2 us (2%)
  loops' own time  10.7 us (1%)
    another operation x44, other arithmetic, group_step(): lax.linalg.triangular_solve(system, right_side, left_side=True, lower=Tru...  475 us
    all_gather x8, waiting for transfers between devices, carried_in(): pieces = jax.tree.map(lambda part: lax.all_gather(part, axis), so_far)  76.2 us
    all_gather x1, waiting for transfers between devices, side_by_side(): filled, at, done = (lax.all_gather(both, axis, axis=dim, tiled=True), 0, [])  32.1 us
    squeeze x32, local copies, waits for them, and re-layouts, recurrence(): memory_end, outputs = lax.scan(jax.checkpoint(group_step), memory, stacked)  26 us
    dot_general x26, matrix products, compose(): jnp.einsum('hij,hjk->hik', later[0], earlier[1], precision=precise)  23 us
    all_gather x4, blocking collectives, carried_in(): pieces = jax.tree.map(lambda part: lax.all_gather(part, axis), so_far)  19.3 us
  transfers between devices with their start and end apart: 11, of which 7 were waited for; matrix products, arithmetic and copies ran while one was open for 53% of the time, Pallas kernels for 0%

commit v1 on v0

v1 whole, which is shorter than its diff:
```python
import jax
import jax.numpy as jnp
from jax import lax
from jax.experimental import pallas as pl
from jax.experimental.pallas import tpu as pltpu
from jax.sharding import Mesh
from jax.sharding import PartitionSpec as P

HEAD_DIM = 128
GROUP = 64
REFL = 2 * GROUP
CTX = ("ctx_0", "ctx_1", "ctx_2")
ROW = ("ctx_1", "ctx_2")
CTX_HEAD = ("ctx_0", "ctx_1", "ctx_2", "head")
F32 = jnp.float32
BF16 = jnp.bfloat16
epsilon = 1e-06


def dot1(a, b, ca, cb):
    return lax.dot_general(a, b, (((ca,), (cb,)), ((), ())), preferred_element_type=F32)


def split(x):
    high = x.astype(BF16)
    return high, (x - high.astype(F32)).astype(BF16)


def mm(a, b, ca=1, cb=0):
    ah, al = split(a)
    bh, bl = split(b)
    return dot1(ah, bh, ca, cb) + (dot1(ah, bl, ca, cb) + dot1(al, bh, ca, cb))


def iota2(rows, cols, dim):
    return lax.broadcasted_iota(jnp.int32, (rows, cols), dim)


def refl_pos(index):
    return 2 * (index % GROUP) + index // GROUP


def unit_scale(raw):
    return 1.0 / jnp.sqrt(jnp.sum(raw * raw, axis=-1, keepdims=True) + epsilon)


class Masks:
    def __init__(self, rows_ref, cols_ref, groups):
        self.pr = refl_pos(iota2(REFL, REFL, 0))
        self.pc = refl_pos(iota2(REFL, REFL, 1))
        self.eye = (self.pr == self.pc).astype(F32)
        self.before = self.pc < self.pr
        tok = iota2(GROUP, REFL, 0)
        self.reach = (iota2(GROUP, REFL, 1) % GROUP) <= tok
        self.rows = rows_ref[...]
        self.cols = cols_ref[...]
        self.groups = groups

    def of(self, g):
        dc = self.cols[g * REFL : (g + 1) * REFL, :]
        dr = self.rows[g : g + 1, :]
        prev = self.rows[self.groups + g : self.groups + g + 1, :]
        last = self.rows[2 * self.groups + g : 2 * self.groups + g + 1, :]
        strict = jnp.logical_and(self.before, dc == dr)
        visible = jnp.logical_and(self.reach, dc[:GROUP] == dr)
        incoming = (dc == prev).astype(F32)
        tail = (dc == last).astype(F32)
        keep = (last == prev).astype(F32)
        return strict, visible, incoming, tail, keep

    def level(self, s):
        same = (self.pr // (2 * s)) == (self.pc // (2 * s))
        return jnp.logical_and(
            same, jnp.logical_and((self.pr // s) % 2 == 1, (self.pc // s) % 2 == 0)
        )


def group_rows(x, g):
    return x[g * GROUP : (g + 1) * GROUP, :]


def transform_kernel(
    tok_ref, wq_ref, wk1_ref, wk2_ref, wv1_ref, wv2_ref, rows_ref, cols_ref,
    q_ref, k1_ref, k2_ref, t_ref, x_ref, s_ref, qt_ref, ol_ref, y_ref, send_ref,
):
    tok = tok_ref[...]
    groups = tok.shape[0] // GROUP
    q = dot1(tok, wq_ref[...], 1, 0)
    k1 = dot1(tok, wk1_ref[...], 1, 0)
    k2 = dot1(tok, wk2_ref[...], 1, 0)
    v1 = dot1(tok, wv1_ref[...], 1, 0)
    v2 = dot1(tok, wv2_ref[...], 1, 0)
    q_ref[...] = q
    k1_ref[...] = k1
    k2_ref[...] = k2
    u1 = k1 * unit_scale(k1)
    u2 = k2 * unit_scale(k2)
    masks = Masks(rows_ref, cols_ref, groups)
    every = range(groups)
    per = [masks.of(g) for g in every]
    keys = [jnp.concatenate([group_rows(u1, g), group_rows(u2, g)], axis=0) for g in every]
    vals = [jnp.concatenate([group_rows(v1, g), group_rows(v2, g)], axis=0) for g in every]
    lows = [jnp.where(per[g][0], 2.0 * mm(keys[g], keys[g], 1, 1), 0.0) for g in every]
    first = masks.level(1)
    inv = [masks.eye - jnp.where(first, lows[g], 0.0) for g in every]
    s = 2
    while s < REFL:
        at = masks.level(s)
        half = [mm(inv[g], jnp.where(at, lows[g], 0.0)) for g in every]
        inv = [inv[g] - mm(half[g], inv[g]) for g in every]
        s *= 2
    total = None
    for g in every:
        strict, visible, incoming, tail, keep = per[g]
        right = jnp.concatenate([2.0 * incoming * keys[g], 2.0 * vals[g]], axis=1)
        x = mm(inv[g], right)
        qg = group_rows(q, g)
        scores = jnp.where(visible, mm(qg, keys[g], 1, 1), 0.0)
        sx = mm(scores, x)
        t_ref[0, g] = inv[g]
        x_ref[0, g] = x
        s_ref[0, g] = scores
        qt_ref[g * GROUP : (g + 1) * GROUP, :] = incoming[:GROUP] * qg - sx[:, :HEAD_DIM]
        ol_ref[g * GROUP : (g + 1) * GROUP, :] = sx[:, HEAD_DIM:]
        xk = mm(x, keys[g] * tail, 0, 0)
        plain = (iota2(HEAD_DIM, HEAD_DIM, 0) == iota2(HEAD_DIM, HEAD_DIM, 1)).astype(F32)
        trans = keep * plain - xk[:HEAD_DIM]
        shift = xk[HEAD_DIM:]
        y_ref[0, g] = jnp.concatenate([trans, shift], axis=0)
        if total is None:
            total = jnp.concatenate([trans, shift], axis=0)
        else:
            total = mm(total, trans)
            total = jnp.concatenate([total[:HEAD_DIM], total[HEAD_DIM:] + shift], axis=0)
    parts = send_ref.shape[0]
    cut = HEAD_DIM // parts
    for j in range(parts):
        send_ref[j, :HEAD_DIM, :] = total[:HEAD_DIM]
        send_ref[j, HEAD_DIM:, :] = total[HEAD_DIM + j * cut : HEAD_DIM + (j + 1) * cut]


def state_kernel(
    n0_ref, y_ref, qt_ref, ol_ref, gn_ref, n_ref, normed_ref, do_ref, e_ref, c_ref
):
    groups = y_ref.shape[1]
    state = n0_ref[0]
    ends = []
    for g in range(groups):
        n_ref[0, g] = state
        qt = qt_ref[g * GROUP : (g + 1) * GROUP, :]
        mixed = ol_ref[g * GROUP : (g + 1) * GROUP, :] + mm(qt, state, 1, 1)
        inv_rms = lax.rsqrt(jnp.mean(mixed * mixed, axis=-1, keepdims=True) + epsilon)
        normal = mixed * inv_rms
        normed_ref[g * GROUP : (g + 1) * GROUP, :] = normal.astype(BF16)
        gn = gn_ref[g * GROUP : (g + 1) * GROUP, :]
        do = inv_rms * (gn - normal * jnp.mean(gn * normal, axis=-1, keepdims=True))
        do_ref[g * GROUP : (g + 1) * GROUP, :] = do
        end = mm(do, qt, 0, 0)
        e_ref[0, g] = end
        ends.append(end)
        if g + 1 < groups:
            state = mm(state, y_ref[0, g, :HEAD_DIM]) + y_ref[0, g, HEAD_DIM:]
    back = ends[groups - 1]
    for g in reversed(range(groups - 1)):
        back = mm(back, y_ref[0, g, :HEAD_DIM], 1, 1) + ends[g]
    c_ref[0] = back


def backward_kernel(
    dn_ref, y_ref, e_ref, n_ref, x_ref, s_ref, t_ref, q_ref, k1_ref, k2_ref, do_ref,
    rows_ref, cols_ref, wq_ref, wk1_ref, wk2_ref, wv1_ref, wv2_ref, out_ref, acc_ref,
):
    groups = y_ref.shape[1]
    masks = Masks(rows_ref, cols_ref, groups)
    every = range(groups)
    after = [None] * groups
    grad_state = dn_ref[0]
    for g in reversed(every):
        after[g] = grad_state
        if g:
            grad_state = mm(grad_state, y_ref[0, g, :HEAD_DIM], 1, 1) + e_ref[0, g]
    k1 = k1_ref[...]
    k2 = k2_ref[...]
    r1 = unit_scale(k1)
    r2 = unit_scale(k2)
    u1 = k1 * r1
    u2 = k2 * r2
    parts = ([], [], [], [], [])
    for g in every:
        strict, visible, incoming, tail, keep = masks.of(g)
        keys = jnp.concatenate([group_rows(u1, g), group_rows(u2, g)], axis=0)
        scale = jnp.concatenate([group_rows(r1, g), group_rows(r2, g)], axis=0)
        state = n_ref[0, g]
        do = do_ref[g * GROUP : (g + 1) * GROUP, :]
        qg = q_ref[g * GROUP : (g + 1) * GROUP, :]
        upd = x_ref[0, g, :, HEAD_DIM:] - mm(x_ref[0, g, :, :HEAD_DIM], state, 1, 1)
        d_upd = mm(s_ref[0, g], do, 0, 0) + mm(keys * tail, after[g], 1, 1)
        d_right = mm(t_ref[0, g], d_upd, 0, 0)
        d_scores = jnp.where(visible, mm(do, upd, 1, 1), 0.0)
        d_gram = jnp.where(strict, -2.0 * mm(d_right, upd, 1, 1), 0.0)
        d_keys = (
            mm(d_gram, keys)
            + mm(d_gram, keys, 0, 0)
            + mm(-2.0 * incoming * d_right, state)
            + mm(d_scores, qg, 0, 0)
            + tail * mm(upd, after[g])
        )
        d_q = mm(d_scores, keys) + incoming[:GROUP] * mm(do, state)
        d_raw = scale * (d_keys - keys * jnp.sum(keys * d_keys, axis=-1, keepdims=True))
        d_val = 2.0 * d_right
        for part, piece in zip(
            parts, (d_q, d_raw[:GROUP], d_raw[GROUP:], d_val[:GROUP], d_val[GROUP:])
        ):
            part.append(piece)
    summed = None
    for part, w_ref in zip(parts, (wq_ref, wk1_ref, wk2_ref, wv1_ref, wv2_ref)):
        piece = dot1(jnp.concatenate(part, axis=0).astype(BF16), w_ref[...], 1, 1)
        summed = piece if summed is None else summed + piece
    h = pl.program_id(0)

    @pl.when(h == 0)
    def _():
        acc_ref[...] = summed

    @pl.when(h > 0)
    def _():
        acc_ref[...] += summed

    @pl.when(h == pl.num_programs(0) - 1)
    def _():
        out_ref[...] = acc_ref[...].astype(BF16)


def row_chain_kernel(in_ref, out_ref):
    total = in_ref[0]
    out_ref[0] = total
    for d in range(1, in_ref.shape[0]):
        here = in_ref[d]
        total = mm(total, here[:HEAD_DIM])
        total = jnp.concatenate([total[:HEAD_DIM], total[HEAD_DIM:] + here[HEAD_DIM:]], axis=0)
        out_ref[d] = total


def row_states_kernel(at_ref, planes_ref, prefix_ref, out_ref):
    at = at_ref[0]
    state = jnp.zeros((planes_ref.shape[1] - HEAD_DIM, HEAD_DIM), F32)
    for k in range(planes_ref.shape[0] - 1):
        there = planes_ref[k]
        new = mm(state, there[:HEAD_DIM]) + there[HEAD_DIM:]
        state = jnp.where(k < at, new, state)
    out_ref[0] = state
    for d in range(1, prefix_ref.shape[0]):
        out_ref[d] = mm(state, prefix_ref[d - 1, :HEAD_DIM]) + prefix_ref[d - 1, HEAD_DIM:]


def row_back_kernel(in_ref, c_ref, out_ref):
    count = in_ref.shape[0]
    back = c_ref[count - 1]
    for d in reversed(range(count - 1)):
        back = mm(back, in_ref[d, :HEAD_DIM], 1, 1) + c_ref[d]
    out_ref[...] = back


def row_grads_kernel(at_ref, planes_ref, c_planes_ref, in_ref, c_ref, out_ref):
    at = at_ref[0]
    grad = jnp.zeros(c_planes_ref.shape[1:], F32)
    for k in reversed(range(1, planes_ref.shape[0])):
        new = mm(grad, planes_ref[k, :HEAD_DIM], 1, 1) + c_planes_ref[k]
        grad = jnp.where(k > at, new, grad)
    for d in reversed(range(in_ref.shape[0])):
        out_ref[d] = grad
        if d:
            grad = mm(grad, in_ref[d, :HEAD_DIM], 1, 1) + c_ref[d]


def whole(kernel, out_shape, *args, scalar=False):
    specs = [pl.BlockSpec(memory_space=pltpu.VMEM) for _ in args]
    if scalar:
        specs[0] = pl.BlockSpec(memory_space=pltpu.SMEM)
    return pl.pallas_call(
        kernel,
        out_shape=jax.ShapeDtypeStruct(out_shape, F32),
        in_specs=specs,
        out_specs=pl.BlockSpec(memory_space=pltpu.VMEM),
    )(*args)


def lane_block(rows):
    return pl.BlockSpec((rows, HEAD_DIM), lambda h: (0, h))


def per_head(*dims):
    return pl.BlockSpec((1, *dims), lambda h: (h,) + (0,) * len(dims))


def fixed(*dims):
    return pl.BlockSpec(dims, lambda h: (0,) * len(dims))


def document_marks(lengths, base, rows):
    doc_first = jnp.cumsum(lengths) - lengths
    groups = rows // GROUP

    def doc_of(positions):
        return jnp.sum(positions[..., None] >= doc_first, axis=-1).astype(F32)

    here = doc_of(base + jnp.arange(rows, dtype=jnp.int32)).reshape(groups, GROUP)
    starts = base + GROUP * jnp.arange(groups, dtype=jnp.int32)
    twice = jnp.concatenate([here, here], axis=1)
    prev = jnp.broadcast_to(doc_of(starts - 1)[:, None], (groups, REFL))
    last = jnp.broadcast_to(doc_of(starts + GROUP - 1)[:, None], (groups, REFL))
    rows_mark = jnp.concatenate([twice, prev, last, jnp.zeros_like(last)], axis=0)
    cols_mark = jnp.broadcast_to(twice.reshape(groups * REFL, 1), (groups * REFL, HEAD_DIM))
    return rows_mark, cols_mark


def sum_at_owner(value, axis):
    count = lax.axis_size(axis)
    pieces = value.reshape(count, value.shape[0] // count, value.shape[1])
    arrived = lax.all_to_all(pieces, axis, split_axis=0, concat_axis=0, tiled=True)
    return arrived.astype(F32).sum(axis=0).astype(BF16)


def per_device(
    tokens, w_query, w_key_first, w_key_second, w_value_first, w_value_second, w_out,
    lengths, out_cotangent,
):
    weights = (w_query, w_key_first, w_key_second, w_value_first, w_value_second)
    token_rows = lax.all_gather(tokens, "head", axis=0, tiled=True)
    cotangent_rows = lax.all_gather(out_cotangent, "head", axis=0, tiled=True)
    rows, width = token_rows.shape
    local = w_query.shape[1]
    heads = local // HEAD_DIM
    groups = rows // GROUP
    row_size = lax.axis_size(ROW)
    parts = row_size // heads
    cut = HEAD_DIM // parts
    rows_mark, cols_mark = document_marks(lengths, lax.axis_index(CTX) * rows, rows)
    plane_at = lax.axis_index("ctx_0").astype(jnp.int32).reshape(1)

    def shape(*dims):
        return jax.ShapeDtypeStruct(dims, F32)

    w_specs = [pl.BlockSpec((width, HEAD_DIM), lambda h: (0, h)) for _ in weights]
    params = pltpu.CompilerParams(dimension_semantics=("arbitrary",))
    q, k1, k2, inverse, x, scores, reach, local_out, steps, send = pl.pallas_call(
        transform_kernel,
        grid=(heads,),
        in_specs=[fixed(rows, width), *w_specs, fixed(*rows_mark.shape), fixed(*cols_mark.shape)],
        out_specs=[
            lane_block(rows), lane_block(rows), lane_block(rows),
            per_head(groups, REFL, REFL), per_head(groups, REFL, 2 * HEAD_DIM),
            per_head(groups, GROUP, REFL), lane_block(rows), lane_block(rows),
            per_head(groups, 2 * HEAD_DIM, HEAD_DIM),
            pl.BlockSpec((parts, HEAD_DIM + cut, HEAD_DIM), lambda h: (h, 0, 0)),
        ],
        out_shape=[
            shape(rows, local), shape(rows, local), shape(rows, local),
            shape(heads, groups, REFL, REFL), shape(heads, groups, REFL, 2 * HEAD_DIM),
            shape(heads, groups, GROUP, REFL), shape(rows, local), shape(rows, local),
            shape(heads, groups, 2 * HEAD_DIM, HEAD_DIM),
            shape(row_size, HEAD_DIM + cut, HEAD_DIM),
        ],
        compiler_params=params,
        name="transform",
    )(token_rows, *weights, rows_mark, cols_mark)

    owned = lax.all_to_all(send, ROW, split_axis=0, concat_axis=0, tiled=True)
    prefix = whole(row_chain_kernel, owned.shape, owned)
    planes = lax.all_gather(prefix[row_size - 1], "ctx_0")
    row_states = whole(
        row_states_kernel, (row_size, cut, HEAD_DIM), plane_at, planes, prefix, scalar=True
    )
    start = lax.all_to_all(row_states, ROW, split_axis=0, concat_axis=0, tiled=True)
    start = start.reshape(heads, HEAD_DIM, HEAD_DIM)
    grad_normed = dot1(cotangent_rows, w_out, 1, 1)

    states, normed, grad_mixed, ends, carried = pl.pallas_call(
        state_kernel,
        grid=(heads,),
        in_specs=[
            per_head(HEAD_DIM, HEAD_DIM), per_head(groups, 2 * HEAD_DIM, HEAD_DIM),
            lane_block(rows), lane_block(rows), lane_block(rows),
        ],
        out_specs=[
            per_head(groups, HEAD_DIM, HEAD_DIM), lane_block(rows), lane_block(rows),
            per_head(groups, HEAD_DIM, HEAD_DIM), per_head(HEAD_DIM, HEAD_DIM),
        ],
        out_shape=[
            shape(heads, groups, HEAD_DIM, HEAD_DIM),
            jax.ShapeDtypeStruct((rows, local), BF16), shape(rows, local),
            shape(heads, groups, HEAD_DIM, HEAD_DIM), shape(heads, HEAD_DIM, HEAD_DIM),
        ],
        compiler_params=params,
        name="state",
    )(start, steps, reach, local_out, grad_normed)

    owned_back = lax.all_to_all(
        carried.reshape(row_size, cut, HEAD_DIM), ROW, split_axis=0, concat_axis=0, tiled=True
    )
    plane_back = whole(row_back_kernel, (cut, HEAD_DIM), owned, owned_back)
    back_planes = lax.all_gather(plane_back, "ctx_0")
    row_grads = whole(
        row_grads_kernel, (row_size, cut, HEAD_DIM),
        plane_at, planes, back_planes, owned, owned_back, scalar=True,
    )
    end_grad = lax.all_to_all(row_grads, ROW, split_axis=0, concat_axis=0, tiled=True)
    end_grad = end_grad.reshape(heads, HEAD_DIM, HEAD_DIM)

    result = sum_at_owner(dot1(normed, w_out, 1, 0).astype(BF16), "head")

    summed = pl.pallas_call(
        backward_kernel,
        grid=(heads,),
        in_specs=[
            per_head(HEAD_DIM, HEAD_DIM), per_head(groups, 2 * HEAD_DIM, HEAD_DIM),
            per_head(groups, HEAD_DIM, HEAD_DIM), per_head(groups, HEAD_DIM, HEAD_DIM),
            per_head(groups, REFL, 2 * HEAD_DIM), per_head(groups, GROUP, REFL),
            per_head(groups, REFL, REFL), lane_block(rows), lane_block(rows), lane_block(rows),
            lane_block(rows), fixed(*rows_mark.shape), fixed(*cols_mark.shape), *w_specs,
        ],
        out_specs=fixed(rows, width),
        out_shape=jax.ShapeDtypeStruct((rows, width), BF16),
        scratch_shapes=[pltpu.VMEM((rows, width), F32)],
        compiler_params=params,
        name="backward",
    )(
        end_grad, steps, ends, states, x, scores, inverse, q, k1, k2, grad_mixed,
        rows_mark, cols_mark, *weights,
    )
    return (result, sum_at_owner(summed, "head"))


def solution(mesh):
    finer = Mesh(
        mesh.devices.reshape(4, 4, 2, mesh.shape["head"]), ("ctx_0", "ctx_1", "ctx_2", "head")
    )
    placed = (
        P(CTX_HEAD, None),
        P(None, "head"),
        P(None, "head"),
        P(None, "head"),
        P(None, "head"),
        P(None, "head"),
        P("head", None),
        P(),
        P(CTX_HEAD, None),
    )
    return jax.shard_map(
        per_device,
        mesh=finer,
        in_specs=placed,
        out_specs=(P(CTX_HEAD, None), P(CTX_HEAD, None)),
        check_vma=False,
    )
```

time: 961 us -> 232 us (0.24); the launches traced: 950 us -> 231 us
  other arithmetic: 521 us -> 4.98 us
  matrix products: 160 us -> 4.58 us
  local copies, waits for them, and re-layouts: 93.8 us -> 3.5 us
  Pallas kernels: 0 us -> 81.2 us
  waiting for transfers between devices: 120 us -> 50.2 us
  blocking collectives: 19.3 us -> 56.8 us
  loops' own time: 10.7 us -> 0 us
    another operation x86 -> x2, other arithmetic: 483 us -> 0.15 us  [the longest x44 475 us: group_step(): lax.linalg.triangular_solve(system, right_side, left_side=True, lower=Tru...]
    dot_general x156 -> x2, matrix products: 145 us -> 4.58 us  [dot1(): lax.dot_general(a, b, (((ca,), (cb,)), ((), ())), preferred_element_type=...]
    all_gather x9 -> x2, waiting for transfers between devices: 108 us -> 24.8 us  [the longest x1 24.7 us: per_device(): token_rows = lax.all_gather(tokens, 'head', axis=0, tiled=True)]
    pallas_call x0 -> x7, Pallas kernels: none -> 81.2 us  [the longest x1 27.3 us: per_device(): pl.pallas_call(transform_kernel, grid=(heads,), in_specs=[fixed(rows, wid...]
    all_to_all x0 -> x2, blocking collectives: none -> 29.3 us  [the longest x1 17.6 us: per_device(): owned = lax.all_to_all(send, ROW, split_axis=0, concat_axis=0, tiled=True)]
    squeeze x32 -> x0, local copies, waits for them, and re-layouts: 26 us -> none  [recurrence(): memory_end, outputs = lax.scan(jax.checkpoint(group_step), memory, stacked)]
    another operation x20 -> x0, matrix products: 15 us -> none  [group_step(): lax.linalg.triangular_solve(system, right_side, left_side=True, lower=Tru...]
    another operation x51 -> x1, local copies, waits for them, and re-layouts: 15.2 us -> 0.73 us  [the longest x5 7.71 us: blockify(): return array_in.reshape((blocks, block_len) + array_in.shape[1:])]
  transfers between devices with their start and end apart: 11 -> 6, of which waited for: 7 -> 4; matrix products, arithmetic and copies ran while one was open for 53% -> 4% of each run, Pallas kernels for 0% -> 26%
where the time goes in v1:
time: 232 us; the launch traced here: 231 us
  Pallas kernels  81.2 us (35%)
  blocking collectives  56.8 us (24%)
  waiting for transfers between devices  50.2 us (22%)
  starting transfers between devices  15.2 us (7%)
  between operations  14.2 us (6%)
  other arithmetic  4.98 us (2%)
  matrix products  4.58 us (2%)
  local copies, waits for them, and re-layouts  3.5 us (2%)
    pallas_call x1, Pallas kernels, per_device(): pl.pallas_call(transform_kernel, grid=(heads,), in_specs=[fixed(rows, wid...  27.3 us
    pallas_call x1, Pallas kernels, per_device(): pl.pallas_call(backward_kernel, grid=(heads,), in_specs=[per_head(HEAD_DI...  26.4 us
    all_gather x1, waiting for transfers between devices, per_device(): token_rows = lax.all_gather(tokens, 'head', axis=0, tiled=True)  24.7 us
    all_to_all x1, blocking collectives, per_device(): owned = lax.all_to_all(send, ROW, split_axis=0, concat_axis=0, tiled=True)  17.6 us
    pallas_call x1, Pallas kernels, per_device(): pl.pallas_call(state_kernel, grid=(heads,), in_specs=[per_head(HEAD_DIM,...  14.3 us
    all_gather x1, blocking collectives, per_device(): back_planes = lax.all_gather(plane_back, 'ctx_0')  13.9 us
    all_to_all x2, waiting for transfers between devices, sum_at_owner(): lax.all_to_all(pieces, axis, split_axis=0, concat_axis=0, tiled=True)  13.8 us
    all_gather x1, blocking collectives, per_device(): planes = lax.all_gather(prefix[row_size - 1], 'ctx_0')  13.5 us
  transfers between devices with their start and end apart: 6, of which 4 were waited for; matrix products, arithmetic and copies ran while one was open for 4% of the time, Pallas kernels for 26%

profile of v1, /device:TPU:0, one launch (start us, length us, event | category | flops | bytes accessed | tf_op | source)
XLA Modules:
  0.0 230.6 jit_solution(16762236160389614864)
XLA Ops:
  11.6 24.7 %all-gather.4.cloned.1.call-done.tok_ref = bf16[256,2048]{1,0:T(8,128)(2,1)} async-done(((bf16[64,2048]{1,0:T(8,128)(2,1)}), bf16[256,2048]{1,0:T(8,128)(2,1)}) %all-gather.4.cloned.1.call-update) | async-done | bytes 1048592 | tf_op jit(solution)/shard_map/all_gather | solution.py:329
  37.2 27.3 %transform.1 = (f32[256,512]{1,0:T(8,128)}, f32[256,512]{1,0:T(8,128)}, f32[256,512]{1,0:T(8,128)}, f32[4,4,128,128]{3,2,1,0:T(8,128)}, f32[4,4,128,256]{3,2,1,0...) custom-call(bf16[256,2048]{1,0:T(8,128)(2,1)} %all-gather.4.cloned.1, ...), custom_call_target="tpu_custom_call" | custom-call | tf_op jit(solution)/shard_map/transform/pallas_call | solution.py:346
  64.5 17.6 %all_to_all.30.in_ref = f32[8,192,128]{2,1,0:T(8,128)} all-to-all(f32[8,192,128]{2,1,0:T(8,128)} %get-tuple-element.17), channel_id=1, replica_groups=mesh['ctx_0'=4,'ctx_1'=4,'ctx_2'=2,'head'=4] {'ctx_1','ctx_2'}, dimensions={0} | all-to-all | bytes 1572864 | tf_op jit(solution)/shard_map/all_to_all | solution.py:368
  82.1 3.3 %shard_map.104.prefix_ref = f32[8,192,128]{2,1,0:T(8,128)} custom-call(f32[8,192,128]{2,1,0:T(8,128)} %all_to_all.30.in_ref), custom_call_target="tpu_custom_call" | custom-call | tf_op jit(solution)/shard_map/pallas_call | solution.py:280
  85.4 0.9 slice.4
  86.3 13.5 %all_gather.16.planes_ref = f32[4,192,128]{2,1,0:T(8,128)} all-gather(f32[1,192,128]{2,1,0:T(8,128)S(1)} %slice.4), channel_id=1, replica_groups=mesh['ctx_0'=4,'ctx_1'=4,'ctx_2'=2,'head'=4] {'ctx_0'}, dimensions={0}, use_global_device_ids=true | all-gather | bytes 491520 | tf_op jit(solution)/shard_map/all_gather | solution.py:370
  99.8 2.8 %shard_map.105 = f32[8,64,128]{2,1,0:T(8,128)} custom-call(s32[1]{0:T(128)} %bitcast.at_ref, f32[4,192,128]{2,1,0:T(8,128)} %all_gather.16.planes_ref, f32[8,192,128]{2,1,0:T(8,128)} %shard_map.104.prefix_ref), custom_call_target="tpu_custom_call" | custom-call | tf_op jit(solution)/shard_map/pallas_call | solution.py:280
  102.6 3.4 %all-to-all-start.1 = ((f32[8,64,128]{2,1,0:T(8,128)}), f32[8,64,128]{2,1,0:T(8,128)S(1)}, u32[]{:S(2)}, u32[]{:S(2)}) async-start(f32[8,64,128]{2,1,0:T(8,128)} %shard_map.105), calls=%async_computation.1 | async-start | bytes 524288 | tf_op jit(solution)/shard_map/all_to_all | solution.py:374
  106.0 2.8 %fusion.2.gn_ref = f32[256,512]{1,0:T(8,128)} fusion(bf16[256,2048]{1,0:T(8,128)(2,1)} %all-gather.6.cloned.1.call-done, bf16[512,2048]{1,0:T(8,128)(2,1)S(1)} %copy-done), kind=kOutput, calls=%fused_computation.10 | convolution fusion | flops 536870912 | bytes 3670016 | tf_op jit(solution)/shard_map/dot_general | solution.py:21
  108.9 4.6 %all-to-all-done.1 = f32[8,64,128]{2,1,0:T(8,128)S(1)} async-done(((f32[8,64,128]{2,1,0:T(8,128)}), f32[8,64,128]{2,1,0:T(8,128)S(1)}, u32[]{:S(2)}, u32[]{:S(2)}) %all-to-all-start.1) | async-done | bytes 262176 | tf_op jit(solution)/shard_map/all_to_all | solution.py:374
  114.2 14.3 %state.1 = (f32[4,4,128,128]{3,2,1,0:T(8,128)}, bf16[256,512]{1,0:T(8,128)(2,1)}, f32[256,512]{1,0:T(8,128)}, f32[4,4,128,128]{3,2,1,0:T(8,128)}, f32[4,128,128]{2,1,0:T(8,128)}) custom-call(f32[4,128,128]{2,1,0:T(8,128)} %bitcast.17, f32[4,4,256,128]{3,2,1,0:T(8,128)} %get-tuple-element.18.y_ref, f32[256,512]{1,0:T(8,128)} %get-tuple-element.19.qt_ref, ...), custom_call_target="tpu_custom_call" | custom-call | tf_op jit(solution)/shard_map/state/pallas_call | solution.py:378
  128.5 11.7 %all_to_all.31.c_ref = f32[8,64,128]{2,1,0:T(8,128)} all-to-all(f32[8,64,128]{2,1,0:T(8,128)} %bitcast.19), channel_id=1, replica_groups=mesh['ctx_0'=4,'ctx_1'=4,'ctx_2'=2,'head'=4] {'ctx_1','ctx_2'}, dimensions={0} | all-to-all | bytes 524288 | tf_op jit(solution)/shard_map/all_to_all | solution.py:398
  140.2 3.1 %shard_map.106 = f32[64,128]{1,0:T(8,128)} custom-call(f32[8,192,128]{2,1,0:T(8,128)} %all_to_all.30.in_ref, f32[8,64,128]{2,1,0:T(8,128)} %all_to_all.31.c_ref), custom_call_target="tpu_custom_call" | custom-call | tf_op jit(solution)/shard_map/pallas_call | solution.py:280
  143.3 13.9 %all-gather = f32[256,128]{1,0:T(8,128)} all-gather(f32[64,128]{1,0:T(8,128)} %shard_map.106), channel_id=2, replica_groups=mesh['ctx_0'=4,'ctx_1'=4,'ctx_2'=2,'head'=4] {'ctx_0'}, dimensions={0}, use_global_device_ids=true | all-gather | bytes 163840 | tf_op jit(solution)/shard_map/all_gather | solution.py:402
  157.2 4.0 %shard_map.107 = f32[8,64,128]{2,1,0:T(8,128)} custom-call(s32[1]{0:T(128)} %bitcast.at_ref, f32[4,192,128]{2,1,0:T(8,128)} %all_gather.16.planes_ref, f32[4,64,128]{2,1,0:T(8,128)} %bitcast.18, f32[8,192,128]{2,1,0:T(8,128)} %all_to_all.30.in_ref, f32[8,64,128]{2,1,0:T(8,128)} %all_to_all.31.c_ref), custom_call_target="tpu_custom_call" | custom-call | tf_op jit(solution)/shard_map/pallas_call | solution.py:280
  161.2 3.4 %all-to-all-start.4 = ((f32[8,64,128]{2,1,0:T(8,128)}), f32[8,64,128]{2,1,0:T(8,128)S(1)}, u32[]{:S(2)}, u32[]{:S(2)}) async-start(f32[8,64,128]{2,1,0:T(8,128)} %shard_map.107), calls=%async_computation.4 | async-start | bytes 524288 | tf_op jit(solution)/shard_map/all_to_all | solution.py:407
  164.7 1.8 convolution_convert_fusion
  166.4 5.7 %all-to-all-done.4 = f32[8,64,128]{2,1,0:T(8,128)S(1)} async-done(((f32[8,64,128]{2,1,0:T(8,128)}), f32[8,64,128]{2,1,0:T(8,128)S(1)}, u32[]{:S(2)}, u32[]{:S(2)}) %all-to-all-start.4) | async-done | bytes 262176 | tf_op jit(solution)/shard_map/all_to_all | solution.py:407
  172.1 3.7 %all-to-all-start.2 = ((bf16[4,64,2048]{2,1,0:T(8,128)(2,1)}), bf16[4,64,2048]{2,1,0:T(8,128)(2,1)S(1)}, u32[]{:S(2)}, u32[]{:S(2)}) async-start(bf16[4,64,2048]{2,1,0:T(8,128)(2,1)} %bitcast.15), calls=%async_computation.2 | async-start | bytes 2097152 | tf_op jit(solution)/shard_map/all_to_all | solution.py:320
  175.8 26.4 %backward.1 = bf16[256,2048]{1,0:T(8,128)(2,1)} custom-call(f32[4,128,128]{2,1,0:T(8,128)} %bitcast.16, f32[4,4,256,128]{3,2,1,0:T(8,128)} %get-tuple-element.18.y_ref, f32[4,4,128,128]{3,2,1,0:T(8,128)} %get-tuple-element.23.e_ref, f32[4,4,128,128]{3,2,1,0:T(8,128)} %get-tuple-element.24.n_ref, f32[4,4,128,256]{3,2,1,0:T(8,128)} %get-tuple-element.25.x_ref, ...), custom_call_target="tpu_custom_call" | custom-call | tf_op jit(solution)/shard_map/backward/pallas_call | solution.py:412
  202.3 4.6 %all-to-all-start.5 = ((bf16[4,64,2048]{2,1,0:T(8,128)(2,1)}), bf16[4,64,2048]{2,1,0:T(8,128)(2,1)}, u32[]{:S(2)}, u32[]{:S(2)}) async-start(bf16[4,64,2048]{2,1,0:T(8,128)(2,1)} %bitcast.14), calls=%async_computation.5 | async-start | bytes 2097152 | tf_op jit(solution)/shard_map/all_to_all | solution.py:320
  206.9 0.9 reduce_sum.54
  207.8 13.8 %all-to-all-done.5 = bf16[4,64,2048]{2,1,0:T(8,128)(2,1)} async-done(((bf16[4,64,2048]{2,1,0:T(8,128)(2,1)}), bf16[4,64,2048]{2,1,0:T(8,128)(2,1)}, u32[]{:S(2)}, u32[]{:S(2)}) %all-to-all-start.5) | async-done | bytes 1048608 | tf_op jit(solution)/shard_map/all_to_all | solution.py:320
  221.6 2.2 reduce_sum.55
  (33 shorter events, 6.0 us)
Async XLA Ops:
  7.2 98.9 %copy-start = (bf16[512,2048]{1,0:T(8,128)(2,1)S(1)}, bf16[512,2048]{1,0:T(8,128)(2,1)}, u32[]{:S(2)}) copy-start(bf16[512,2048]{1,0:T(8,128)(2,1)} %param.15) | copy-start | bytes 6291460
  7.2 29.2 %all-gather.4.cloned.1.call-start = ((), (), s32[]{:S(2)}) async-start(), calls=%async_computation.6 | async-start | bytes 1310720 | tf_op jit(solution)/shard_map/all_gather | solution.py:329
  7.9 98.1 %all-gather.6.cloned.1.call-start = ((), (), s32[]{:S(2)}) async-start(), calls=%async_computation.7 | async-start | bytes 1310720 | tf_op jit(solution)/shard_map/all_gather | solution.py:330
  102.6 10.9 %all-to-all-start.1 = ((f32[8,64,128]{2,1,0:T(8,128)}), f32[8,64,128]{2,1,0:T(8,128)S(1)}, u32[]{:S(2)}, u32[]{:S(2)}) async-start(f32[8,64,128]{2,1,0:T(8,128)} %shard_map.105), calls=%async_computation.1 | async-start | bytes 524288 | tf_op jit(solution)/shard_map/all_to_all | solution.py:374
  113.5 0.7 copy-start.2
  128.5 36.2 %copy-start.3 = (bf16[256,512]{1,0:T(8,128)(2,1)S(1)}, bf16[256,512]{1,0:T(8,128)(2,1)}, u32[]{:S(2)}) copy-start(bf16[256,512]{1,0:T(8,128)(2,1)} %get-tuple-element.21) | copy-start | bytes 786436
  161.2 10.9 %all-to-all-start.4 = ((f32[8,64,128]{2,1,0:T(8,128)}), f32[8,64,128]{2,1,0:T(8,128)S(1)}, u32[]{:S(2)}, u32[]{:S(2)}) async-start(f32[8,64,128]{2,1,0:T(8,128)} %shard_map.107), calls=%async_computation.4 | async-start | bytes 524288 | tf_op jit(solution)/shard_map/all_to_all | solution.py:407
  172.1 3.7 %copy-start.1 = (f32[8,64,128]{2,1,0:T(8,128)}, f32[8,64,128]{2,1,0:T(8,128)S(1)}, u32[]{:S(2)}) copy-start(f32[8,64,128]{2,1,0:T(8,128)S(1)} %all-to-all-done.4) | copy-start | bytes 786436
  172.1 30.1 %all-to-all-start.2 = ((bf16[4,64,2048]{2,1,0:T(8,128)(2,1)}), bf16[4,64,2048]{2,1,0:T(8,128)(2,1)S(1)}, u32[]{:S(2)}, u32[]{:S(2)}) async-start(bf16[4,64,2048]{2,1,0:T(8,128)(2,1)} %bitcast.15), calls=%async_computation.2 | async-start | bytes 2097152 | tf_op jit(solution)/shard_map/all_to_all | solution.py:320
  202.3 19.3 %all-to-all-start.5 = ((bf16[4,64,2048]{2,1,0:T(8,128)(2,1)}), bf16[4,64,2048]{2,1,0:T(8,128)(2,1)}, u32[]{:S(2)}, u32[]{:S(2)}) async-start(bf16[4,64,2048]{2,1,0:T(8,128)(2,1)} %bitcast.14), calls=%async_computation.5 | async-start | bytes 2097152 | tf_op jit(solution)/shard_map/all_to_all | solution.py:320
Sparse Core Ops, SparseCore 0:
  9.7 26.6 all-gather.3
  38.0 24.5 all-gather.5

commit v2 on v1

v2 whole, which is shorter than its diff:
```python
import jax
import jax.numpy as jnp
from jax import lax
from jax.experimental import pallas as pl
from jax.experimental.pallas import tpu as pltpu
from jax.sharding import Mesh
from jax.sharding import PartitionSpec as P

HEAD_DIM = 128
GROUP = 64
REFL = 2 * GROUP
CTX = ("ctx_0", "ctx_1", "ctx_2")
ROW = ("ctx_1", "ctx_2")
CTX_HEAD = ("ctx_0", "ctx_1", "ctx_2", "head")
F32 = jnp.float32
BF16 = jnp.bfloat16
epsilon = 1e-06
HEADS_FIRST = 2
HEADS_STATE = 2
HEADS_BACK = 2
MIB = 1 << 20
LIMIT_FIRST = None
LIMIT_STATE = 57 * MIB
LIMIT_BACK = None
LIMIT_ROW = 6 * MIB


def dot1(a, b, ca, cb):
    return lax.dot_general(a, b, (((ca,), (cb,)), ((), ())), preferred_element_type=F32)


def split(x):
    high = x.astype(BF16)
    return high, (x - high.astype(F32)).astype(BF16)


def mm(a, b, ca=1, cb=0):
    ah, al = split(a)
    bh, bl = split(b)
    if a.shape[ca] % 128:
        return dot1(ah, bh, ca, cb) + (dot1(ah, bl, ca, cb) + dot1(al, bh, ca, cb))
    both = dot1(jnp.concatenate([ah, al], ca), jnp.concatenate([bh, bh], cb), ca, cb)
    return both + dot1(ah, bl, ca, cb)


def iota2(rows, cols, dim):
    return lax.broadcasted_iota(jnp.int32, (rows, cols), dim)


def refl_pos(index):
    return 2 * (index % GROUP) + index // GROUP


def unit_scale(raw):
    return 1.0 / jnp.sqrt(jnp.sum(raw * raw, axis=-1, keepdims=True) + epsilon)


class Masks:
    def __init__(self, rows_ref, cols_ref, groups):
        self.pr = refl_pos(iota2(REFL, REFL, 0))
        self.pc = refl_pos(iota2(REFL, REFL, 1))
        self.eye = (self.pr == self.pc).astype(F32)
        self.before = self.pc < self.pr
        tok = iota2(GROUP, REFL, 0)
        self.reach = (iota2(GROUP, REFL, 1) % GROUP) <= tok
        self.rows = rows_ref[...]
        self.cols = cols_ref[...]
        self.groups = groups

    def of(self, g):
        dc = self.cols[g * REFL : (g + 1) * REFL, :]
        dr = self.rows[g : g + 1, :]
        prev = self.rows[self.groups + g : self.groups + g + 1, :]
        last = self.rows[2 * self.groups + g : 2 * self.groups + g + 1, :]
        strict = jnp.logical_and(self.before, dc == dr)
        visible = jnp.logical_and(self.reach, dc[:GROUP] == dr)
        incoming = (dc == prev).astype(F32)
        tail = (dc == last).astype(F32)
        keep = (last == prev).astype(F32)
        return strict, visible, incoming, tail, keep

    def level(self, s):
        same = (self.pr // (2 * s)) == (self.pc // (2 * s))
        return jnp.logical_and(
            same, jnp.logical_and((self.pr // s) % 2 == 1, (self.pc // s) % 2 == 0)
        )


def group_rows(x, g):
    return x[g * GROUP : (g + 1) * GROUP, :]


def heads_in(ref):
    return range(ref.shape[1] // HEAD_DIM)


def lanes(x, h):
    return x[:, h * HEAD_DIM : (h + 1) * HEAD_DIM]


def transform_kernel(
    at_ref, tok0_ref, tok1_ref, tok2_ref, tok3_ref, wq_ref, wk1_ref, wk2_ref, wv1_ref, wv2_ref,
    rows_ref, cols_ref,
    q_ref, k1_ref, k2_ref, t_ref, x_ref, s_ref, qt_ref, ol_ref, y_ref, send_ref, tok_ref,
):
    at = at_ref[0]

    @pl.when(pl.program_id(0) == 0)
    def _():
        for rel, piece in enumerate((tok0_ref, tok1_ref, tok2_ref, tok3_ref)):
            tok_ref[at ^ rel] = piece[...]

    tok = tok_ref[...].reshape(-1, tok_ref.shape[2])
    groups = tok.shape[0] // GROUP
    q = dot1(tok, wq_ref[...], 1, 0)
    k1 = dot1(tok, wk1_ref[...], 1, 0)
    k2 = dot1(tok, wk2_ref[...], 1, 0)
    v1 = dot1(tok, wv1_ref[...], 1, 0)
    v2 = dot1(tok, wv2_ref[...], 1, 0)
    q_ref[...] = q
    k1_ref[...] = k1
    k2_ref[...] = k2
    masks = Masks(rows_ref, cols_ref, groups)
    per = [masks.of(g) for g in range(groups)]
    plain = (iota2(HEAD_DIM, HEAD_DIM, 0) == iota2(HEAD_DIM, HEAD_DIM, 1)).astype(F32)
    every = [(h, g) for h in heads_in(q_ref) for g in range(groups)]
    unit = [
        (lanes(k1, h) * unit_scale(lanes(k1, h)), lanes(k2, h) * unit_scale(lanes(k2, h)))
        for h in heads_in(q_ref)
    ]
    keys = {
        (h, g): jnp.concatenate([group_rows(unit[h][0], g), group_rows(unit[h][1], g)], axis=0)
        for h, g in every
    }
    lows = {i: jnp.where(per[i[1]][0], 2.0 * mm(keys[i], keys[i], 1, 1), 0.0) for i in every}
    first = masks.level(1)
    inv = {i: masks.eye - jnp.where(first, lows[i], 0.0) for i in every}
    s = 2
    while s < REFL:
        here = masks.level(s)
        half = {i: mm(inv[i], jnp.where(here, lows[i], 0.0)) for i in every}
        inv = {i: inv[i] - mm(half[i], inv[i]) for i in every}
        s *= 2
    trans = {}
    shift = {}
    for i in every:
        h, g = i
        strict, visible, incoming, tail, keep = per[g]
        at_rows = slice(g * GROUP, (g + 1) * GROUP)
        at_lanes = slice(h * HEAD_DIM, (h + 1) * HEAD_DIM)
        vals = jnp.concatenate([lanes(group_rows(v1, g), h), lanes(group_rows(v2, g), h)], axis=0)
        right = jnp.concatenate([2.0 * incoming * keys[i], 2.0 * vals], axis=1)
        x = mm(inv[i], right)
        qg = lanes(group_rows(q, g), h)
        scores = jnp.where(visible, mm(qg, keys[i], 1, 1), 0.0)
        sx = mm(scores, x)
        t_ref[h, g] = inv[i]
        x_ref[h, g] = x
        s_ref[h, g] = scores
        qt_ref[at_rows, at_lanes] = incoming[:GROUP] * qg - sx[:, :HEAD_DIM]
        ol_ref[at_rows, at_lanes] = sx[:, HEAD_DIM:]
        xk = mm(x, keys[i] * tail, 0, 0)
        trans[i] = keep * plain - xk[:HEAD_DIM]
        shift[i] = xk[HEAD_DIM:]
        y_ref[h, g, :HEAD_DIM] = trans[i]
        y_ref[h, g, HEAD_DIM:] = shift[i]
    total = {h: jnp.concatenate([trans[h, 0], shift[h, 0]], axis=0) for h in heads_in(q_ref)}
    for g in range(1, groups):
        for h in heads_in(q_ref):
            new = mm(total[h], trans[h, g])
            total[h] = jnp.concatenate([new[:HEAD_DIM], new[HEAD_DIM:] + shift[h, g]], axis=0)
    parts = send_ref.shape[0] // len(heads_in(q_ref))
    cut = HEAD_DIM // parts
    for h in heads_in(q_ref):
        for j in range(parts):
            send_ref[h * parts + j, :HEAD_DIM, :] = total[h][:HEAD_DIM]
            send_ref[h * parts + j, HEAD_DIM:, :] = total[h][
                HEAD_DIM + j * cut : HEAD_DIM + (j + 1) * cut
            ]


def state_kernel(
    at_ref, n0_ref, y_ref, qt_ref, ol_ref, gn_ref, n_ref, normed_ref, do_ref, e_ref, c_ref
):
    at = at_ref[0]
    groups = y_ref.shape[1]
    heads = heads_in(qt_ref)
    state = {h: n0_ref[h] for h in heads}
    ends = {}
    for g in range(groups):
        at_rows = slice(g * GROUP, (g + 1) * GROUP)
        for h in heads:
            n_ref[h, g] = state[h]
        mixed = {
            h: lanes(ol_ref[at_rows, :], h) + mm(lanes(qt_ref[at_rows, :], h), state[h], 1, 1)
            for h in heads
        }
        if g + 1 < groups:
            state = {
                h: mm(state[h], y_ref[h, g, :HEAD_DIM]) + y_ref[h, g, HEAD_DIM:] for h in heads
            }
        grad_rows = gn_ref[at ^ g]
        for h in heads:
            at_lanes = slice(h * HEAD_DIM, (h + 1) * HEAD_DIM)
            inv_rms = lax.rsqrt(jnp.mean(mixed[h] * mixed[h], axis=-1, keepdims=True) + epsilon)
            normal = mixed[h] * inv_rms
            normed_ref[at_rows, at_lanes] = normal.astype(BF16)
            gn = lanes(grad_rows, h)
            do = inv_rms * (gn - normal * jnp.mean(gn * normal, axis=-1, keepdims=True))
            do_ref[at_rows, at_lanes] = do
            ends[h, g] = mm(do, lanes(qt_ref[at_rows, :], h), 0, 0)
            e_ref[h, g] = ends[h, g]
    back = {h: ends[h, groups - 1] for h in heads}
    for g in reversed(range(groups - 1)):
        back = {h: mm(back[h], y_ref[h, g, :HEAD_DIM], 1, 1) + ends[h, g] for h in heads}
    for h in heads:
        c_ref[h] = back[h]


def backward_kernel(
    at_ref, dn_ref, y_ref, e_ref, n_ref, x_ref, s_ref, t_ref, q_ref, k1_ref, k2_ref, do_ref,
    rows_ref, cols_ref, wq_ref, wk1_ref, wk2_ref, wv1_ref, wv2_ref,
    out0_ref, out1_ref, out2_ref, out3_ref, acc_ref,
):
    at = at_ref[0]
    groups = y_ref.shape[1]
    heads = heads_in(q_ref)
    masks = Masks(rows_ref, cols_ref, groups)
    per = [masks.of(g) for g in range(groups)]
    after = {}
    grad_state = {h: dn_ref[h] for h in heads}
    for g in reversed(range(groups)):
        for h in heads:
            after[h, g] = grad_state[h]
        if g:
            grad_state = {
                h: mm(grad_state[h], y_ref[h, g, :HEAD_DIM], 1, 1) + e_ref[h, g] for h in heads
            }
    parts = ([], [], [], [], [])
    for h in heads:
        k1 = lanes(k1_ref[...], h)
        k2 = lanes(k2_ref[...], h)
        r1 = unit_scale(k1)
        r2 = unit_scale(k2)
        u1 = k1 * r1
        u2 = k2 * r2
        mine = ([], [], [], [], [])
        for g in range(groups):
            strict, visible, incoming, tail, keep = per[g]
            at_rows = slice(g * GROUP, (g + 1) * GROUP)
            keys = jnp.concatenate([group_rows(u1, g), group_rows(u2, g)], axis=0)
            scale = jnp.concatenate([group_rows(r1, g), group_rows(r2, g)], axis=0)
            state = n_ref[h, g]
            do = lanes(do_ref[at_rows, :], h)
            qg = lanes(q_ref[at_rows, :], h)
            upd = x_ref[h, g, :, HEAD_DIM:] - mm(x_ref[h, g, :, :HEAD_DIM], state, 1, 1)
            d_upd = mm(s_ref[h, g], do, 0, 0) + mm(keys * tail, after[h, g], 1, 1)
            d_right = mm(t_ref[h, g], d_upd, 0, 0)
            d_scores = jnp.where(visible, mm(do, upd, 1, 1), 0.0)
            d_gram = jnp.where(strict, -2.0 * mm(d_right, upd, 1, 1), 0.0)
            d_keys = (
                mm(d_gram, keys)
                + mm(d_gram, keys, 0, 0)
                + mm(-2.0 * incoming * d_right, state)
                + mm(d_scores, qg, 0, 0)
                + tail * mm(upd, after[h, g])
            )
            d_q = mm(d_scores, keys) + incoming[:GROUP] * mm(do, state)
            d_raw = scale * (d_keys - keys * jnp.sum(keys * d_keys, axis=-1, keepdims=True))
            d_val = 2.0 * d_right
            pieces = (d_q, d_raw[:GROUP], d_raw[GROUP:], d_val[:GROUP], d_val[GROUP:])
            for part, piece in zip(mine, pieces):
                part.append(piece.astype(BF16))
        for part, piece in zip(parts, mine):
            part.append(jnp.concatenate(piece, axis=0))
    summed = None
    for part, w_ref in zip(parts, (wq_ref, wk1_ref, wk2_ref, wv1_ref, wv2_ref)):
        piece = dot1(jnp.concatenate(part, axis=1), w_ref[...], 1, 1)
        summed = piece if summed is None else summed + piece
    summed = summed.reshape(acc_ref.shape)
    step = pl.program_id(0)

    @pl.when(step == 0)
    def _():
        acc_ref[...] = summed

    @pl.when(step > 0)
    def _():
        acc_ref[...] += summed

    @pl.when(step == pl.num_programs(0) - 1)
    def _():
        for rel, out_ref in enumerate((out0_ref, out1_ref, out2_ref, out3_ref)):
            out_ref[...] = acc_ref[at ^ rel].astype(BF16)


def row_chain_kernel(in_ref, out_ref, last_ref):
    total = in_ref[0]
    out_ref[0] = total
    for d in range(1, in_ref.shape[0]):
        here = in_ref[d]
        total = mm(total, here[:HEAD_DIM])
        total = jnp.concatenate([total[:HEAD_DIM], total[HEAD_DIM:] + here[HEAD_DIM:]], axis=0)
        out_ref[d] = total
    last_ref[...] = total


def row_states_kernel(at_ref, p0_ref, p1_ref, p2_ref, p3_ref, prefix_ref, out_ref, planes_ref):
    at = at_ref[1]
    for rel, piece in enumerate((p0_ref, p1_ref, p2_ref, p3_ref)):
        planes_ref[at ^ rel] = piece[...]
    state = jnp.zeros((planes_ref.shape[1] - HEAD_DIM, HEAD_DIM), F32)
    for k in range(planes_ref.shape[0] - 1):
        there = planes_ref[k]
        new = mm(state, there[:HEAD_DIM]) + there[HEAD_DIM:]
        state = jnp.where(k < at, new, state)
    out_ref[0] = state
    for d in range(1, prefix_ref.shape[0]):
        out_ref[d] = mm(state, prefix_ref[d - 1, :HEAD_DIM]) + prefix_ref[d - 1, HEAD_DIM:]


def row_back_kernel(in_ref, c_ref, out_ref):
    count = in_ref.shape[0]
    back = c_ref[count - 1]
    for d in reversed(range(count - 1)):
        back = mm(back, in_ref[d, :HEAD_DIM], 1, 1) + c_ref[d]
    out_ref[...] = back


def row_grads_kernel(
    at_ref, p0_ref, p1_ref, p2_ref, p3_ref, c0_ref, c1_ref, c2_ref, c3_ref, in_ref, c_ref,
    out_ref, planes_ref,
):
    at = at_ref[1]
    for rel, (piece, tail) in enumerate(
        zip((p0_ref, p1_ref, p2_ref, p3_ref), (c0_ref, c1_ref, c2_ref, c3_ref))
    ):
        planes_ref[at ^ rel, :HEAD_DIM] = piece[:HEAD_DIM]
        planes_ref[at ^ rel, HEAD_DIM:] = tail[...]
    grad = jnp.zeros(c0_ref.shape, F32)
    for k in reversed(range(1, planes_ref.shape[0])):
        new = mm(grad, planes_ref[k, :HEAD_DIM], 1, 1) + planes_ref[k, HEAD_DIM:]
        grad = jnp.where(k > at, new, grad)
    for d in reversed(range(in_ref.shape[0])):
        out_ref[d] = grad
        if d:
            grad = mm(grad, in_ref[d, :HEAD_DIM], 1, 1) + c_ref[d]


def whole(kernel, out_shapes, *args, scalar=False, scratch=()):
    specs = [pl.BlockSpec(memory_space=pltpu.VMEM) for _ in args]
    if scalar:
        specs[0] = pl.BlockSpec(memory_space=pltpu.SMEM)
    return pl.pallas_call(
        kernel,
        out_shape=[jax.ShapeDtypeStruct(dims, F32) for dims in out_shapes],
        in_specs=specs,
        out_specs=[pl.BlockSpec(memory_space=pltpu.VMEM) for _ in out_shapes],
        scratch_shapes=[pltpu.VMEM(dims, F32) for dims in scratch],
        compiler_params=pltpu.CompilerParams(vmem_limit_bytes=LIMIT_ROW),
    )(*args)


def exchanged(value, axis):
    count = lax.axis_size(axis)
    return [value] + [
        lax.ppermute(value, axis, [(j, j ^ rel) for j in range(count)]) for rel in range(1, count)
    ]


def lane_block(rows, heads):
    return pl.BlockSpec((rows, heads * HEAD_DIM), lambda h: (0, h))


def per_head(heads, *dims):
    return pl.BlockSpec((heads, *dims), lambda h: (h,) + (0,) * len(dims))


def fixed(*dims):
    return pl.BlockSpec(dims, lambda h: (0,) * len(dims))


def document_marks(lengths, base, rows):
    doc_first = jnp.cumsum(lengths) - lengths
    groups = rows // GROUP

    def doc_of(positions):
        return jnp.sum(positions[..., None] >= doc_first, axis=-1).astype(F32)

    here = doc_of(base + jnp.arange(rows, dtype=jnp.int32)).reshape(groups, GROUP)
    starts = base + GROUP * jnp.arange(groups, dtype=jnp.int32)
    twice = jnp.concatenate([here, here], axis=1)
    prev = jnp.broadcast_to(doc_of(starts - 1)[:, None], (groups, REFL))
    last = jnp.broadcast_to(doc_of(starts + GROUP - 1)[:, None], (groups, REFL))
    rows_mark = jnp.concatenate([twice, prev, last, jnp.zeros_like(last)], axis=0)
    cols_mark = jnp.broadcast_to(twice.reshape(groups * REFL, 1), (groups * REFL, HEAD_DIM))
    return rows_mark, cols_mark


def sum_at_owner(value, axis):
    count = lax.axis_size(axis)
    pieces = value.reshape(count, value.shape[0] // count, value.shape[1])
    arrived = lax.all_to_all(pieces, axis, split_axis=0, concat_axis=0, tiled=True)
    return arrived.astype(F32).sum(axis=0).astype(BF16)


def per_device(
    tokens, w_query, w_key_first, w_key_second, w_value_first, w_value_second, w_out,
    lengths, out_cotangent,
):
    weights = (w_query, w_key_first, w_key_second, w_value_first, w_value_second)
    shards = lax.axis_size("head")
    token_parts = exchanged(tokens, "head")
    cotangent_parts = exchanged(out_cotangent, "head")
    share, width = tokens.shape
    rows = share * shards
    local = w_query.shape[1]
    heads = local // HEAD_DIM
    groups = rows // GROUP
    row_size = lax.axis_size(ROW)
    parts = row_size // heads
    cut = HEAD_DIM // parts
    rows_mark, cols_mark = document_marks(lengths, lax.axis_index(CTX) * rows, rows)
    at = jnp.stack([lax.axis_index("head"), lax.axis_index("ctx_0")]).astype(jnp.int32)
    scalars = pl.BlockSpec(memory_space=pltpu.SMEM)

    def shape(*dims):
        return jax.ShapeDtypeStruct(dims, F32)

    def w_specs(n):
        return [pl.BlockSpec((width, n * HEAD_DIM), lambda h: (0, h)) for _ in weights]

    def params(limit):
        return pltpu.CompilerParams(
            dimension_semantics=("arbitrary",), vmem_limit_bytes=limit
        )

    n = HEADS_FIRST
    q, k1, k2, inverse, x, scores, reach, local_out, steps, send = pl.pallas_call(
        transform_kernel,
        grid=(heads // n,),
        in_specs=[
            scalars, *[fixed(share, width)] * shards, *w_specs(n),
            fixed(*rows_mark.shape), fixed(*cols_mark.shape),
        ],
        out_specs=[
            lane_block(rows, n), lane_block(rows, n), lane_block(rows, n),
            per_head(n, groups, REFL, REFL), per_head(n, groups, REFL, 2 * HEAD_DIM),
            per_head(n, groups, GROUP, REFL), lane_block(rows, n), lane_block(rows, n),
            per_head(n, groups, 2 * HEAD_DIM, HEAD_DIM),
            per_head(n * parts, HEAD_DIM + cut, HEAD_DIM),
        ],
        out_shape=[
            shape(rows, local), shape(rows, local), shape(rows, local),
            shape(heads, groups, REFL, REFL), shape(heads, groups, REFL, 2 * HEAD_DIM),
            shape(heads, groups, GROUP, REFL), shape(rows, local), shape(rows, local),
            shape(heads, groups, 2 * HEAD_DIM, HEAD_DIM),
            shape(row_size, HEAD_DIM + cut, HEAD_DIM),
        ],
        scratch_shapes=[pltpu.VMEM((shards, share, width), BF16)],
        compiler_params=params(LIMIT_FIRST),
        name="transform",
    )(at, *token_parts, *weights, rows_mark, cols_mark)

    owned = lax.all_to_all(send, ROW, split_axis=0, concat_axis=0, tiled=True)
    prefix, plane = whole(row_chain_kernel, [owned.shape, owned.shape[1:]], owned)
    planes = exchanged(plane, "ctx_0")
    plane_scratch = [(len(planes), *plane.shape)]
    (row_states,) = whole(
        row_states_kernel, [(row_size, cut, HEAD_DIM)], at, *planes, prefix,
        scalar=True, scratch=plane_scratch,
    )
    start = lax.all_to_all(row_states, ROW, split_axis=0, concat_axis=0, tiled=True)
    start = start.reshape(heads, HEAD_DIM, HEAD_DIM)
    grad_normed = dot1(jnp.concatenate(cotangent_parts, axis=0), w_out, 1, 1)

    n = HEADS_STATE
    states, normed, grad_mixed, ends, carried = pl.pallas_call(
        state_kernel,
        grid=(heads // n,),
        in_specs=[
            scalars, per_head(n, HEAD_DIM, HEAD_DIM), per_head(n, groups, 2 * HEAD_DIM, HEAD_DIM),
            lane_block(rows, n), lane_block(rows, n),
            pl.BlockSpec((shards, share, n * HEAD_DIM), lambda h: (0, 0, h)),
        ],
        out_specs=[
            per_head(n, groups, HEAD_DIM, HEAD_DIM), lane_block(rows, n), lane_block(rows, n),
            per_head(n, groups, HEAD_DIM, HEAD_DIM), per_head(n, HEAD_DIM, HEAD_DIM),
        ],
        out_shape=[
            shape(heads, groups, HEAD_DIM, HEAD_DIM),
            jax.ShapeDtypeStruct((rows, local), BF16), shape(rows, local),
            shape(heads, groups, HEAD_DIM, HEAD_DIM), shape(heads, HEAD_DIM, HEAD_DIM),
        ],
        compiler_params=params(LIMIT_STATE),
        name="state",
    )(at, start, steps, reach, local_out, grad_normed.reshape(shards, share, local))

    owned_back = lax.all_to_all(
        carried.reshape(row_size, cut, HEAD_DIM), ROW, split_axis=0, concat_axis=0, tiled=True
    )
    (plane_back,) = whole(row_back_kernel, [(cut, HEAD_DIM)], owned, owned_back)
    back_planes = exchanged(plane_back, "ctx_0")
    (row_grads,) = whole(
        row_grads_kernel, [(row_size, cut, HEAD_DIM)],
        at, *planes, *back_planes, owned, owned_back, scalar=True, scratch=plane_scratch,
    )
    end_grad = lax.all_to_all(row_grads, ROW, split_axis=0, concat_axis=0, tiled=True)
    end_grad = end_grad.reshape(heads, HEAD_DIM, HEAD_DIM)

    result = sum_at_owner(dot1(normed, w_out, 1, 0).astype(BF16), "head")

    n = HEADS_BACK
    summed = pl.pallas_call(
        backward_kernel,
        grid=(heads // n,),
        in_specs=[
            scalars, per_head(n, HEAD_DIM, HEAD_DIM), per_head(n, groups, 2 * HEAD_DIM, HEAD_DIM),
            per_head(n, groups, HEAD_DIM, HEAD_DIM), per_head(n, groups, HEAD_DIM, HEAD_DIM),
            per_head(n, groups, REFL, 2 * HEAD_DIM), per_head(n, groups, GROUP, REFL),
            per_head(n, groups, REFL, REFL), lane_block(rows, n), lane_block(rows, n),
            lane_block(rows, n), lane_block(rows, n),
            fixed(*rows_mark.shape), fixed(*cols_mark.shape), *w_specs(n),
        ],
        out_specs=[fixed(share, width)] * shards,
        out_shape=[jax.ShapeDtypeStruct((share, width), BF16)] * shards,
        scratch_shapes=[pltpu.VMEM((shards, share, width), F32)],
        compiler_params=params(LIMIT_BACK),
        name="backward",
    )(
        at, end_grad, steps, ends, states, x, scores, inverse, q, k1, k2, grad_mixed,
        rows_mark, cols_mark, *weights,
    )
    grad_tokens = summed[0].astype(F32)
    for rel in range(1, shards):
        to_owner = [(j, j ^ rel) for j in range(shards)]
        grad_tokens = grad_tokens + lax.ppermute(summed[rel], "head", to_owner).astype(F32)
    return (result, grad_tokens.astype(BF16))


def solution(mesh):
    finer = Mesh(
        mesh.devices.reshape(4, 4, 2, mesh.shape["head"]), ("ctx_0", "ctx_1", "ctx_2", "head")
    )
    placed = (
        P(CTX_HEAD, None),
        P(None, "head"),
        P(None, "head"),
        P(None, "head"),
        P(None, "head"),
        P(None, "head"),
        P("head", None),
        P(),
        P(CTX_HEAD, None),
    )
    return jax.shard_map(
        per_device,
        mesh=finer,
        in_specs=placed,
        out_specs=(P(CTX_HEAD, None), P(CTX_HEAD, None)),
        check_vma=False,
    )
```

time: 232 us -> 171 us (0.74)
  blocking collectives: 56.8 us -> 10.8 us
  Pallas kernels: 81.2 us -> 55.5 us
  starting transfers between devices: 15.2 us -> 37.7 us
  between operations: 14.2 us -> 0.75 us
    ppermute x0 -> x15, waiting for transfers between devices: none -> 34.2 us  [the longest x12 20.7 us: exchanged(): lax.ppermute(value, axis, [(j, j ^ rel) for j in range(count)])]
    all_gather x2 -> x0, blocking collectives: 27.5 us -> none  [the longest x1 13.9 us: per_device(): back_planes = lax.all_gather(plane_back, 'ctx_0')]
    pallas_call x7, Pallas kernels: 81.2 us -> 55.5 us  [the longest x1 21.9 us: per_device(): pl.pallas_call(backward_kernel, grid=(heads // n,), in_specs=[scalars, pe...]
    all_gather x2 -> x0, waiting for transfers between devices: 24.8 us -> none  [the longest x1 24.7 us: per_device(): token_rows = lax.all_gather(tokens, 'head', axis=0, tiled=True)]
    ppermute x0 -> x15, starting transfers between devices: none -> 22.3 us  [the longest x12 17.5 us: exchanged(): lax.ppermute(value, axis, [(j, j ^ rel) for j in range(count)])]
    all_to_all x1 -> x0, blocking collectives: 17.6 us -> none  [per_device(): owned = lax.all_to_all(send, ROW, split_axis=0, concat_axis=0, tiled=True)]
    all_to_all x2 -> x1, waiting for transfers between devices: 13.8 us -> 0.01 us  [sum_at_owner(): lax.all_to_all(pieces, axis, split_axis=0, concat_axis=0, tiled=True)]
    all_to_all x0 -> x1, waiting for transfers between devices: none -> 9.06 us  [per_device(): owned = lax.all_to_all(send, ROW, split_axis=0, concat_axis=0, tiled=True)]
  transfers between devices with their start and end apart: 6 -> 19, of which waited for: 4 -> 13; matrix products, arithmetic and copies ran while one was open for 4% -> 6% of each run, Pallas kernels for 26% -> 15%
where the time goes in v2:
time: 171 us
  Pallas kernels  55.5 us (32%)
  waiting for transfers between devices  52.5 us (31%)
  starting transfers between devices  37.7 us (22%)
  blocking collectives  10.8 us (6%)
  matrix products  5.43 us (3%)
  other arithmetic  5.16 us (3%)
  local copies, waits for them, and re-layouts  2.65 us (2%)
    pallas_call x1, Pallas kernels, per_device(): pl.pallas_call(backward_kernel, grid=(heads // n,), in_specs=[scalars, pe...  21.9 us
    ppermute x12, waiting for transfers between devices, exchanged(): lax.ppermute(value, axis, [(j, j ^ rel) for j in range(count)])  20.7 us
    pallas_call x1, Pallas kernels, per_device(): pl.pallas_call(transform_kernel, grid=(heads // n,), in_specs=[scalars, *...  19.7 us
    ppermute x12, starting transfers between devices, exchanged(): lax.ppermute(value, axis, [(j, j ^ rel) for j in range(count)])  17.5 us
    ppermute x3, waiting for transfers between devices, per_device(): lax.ppermute(summed[rel], 'head', to_owner).astype(F32)  13.5 us
    all_to_all x1, blocking collectives, per_device(): lax.all_to_all(carried.reshape(row_size, cut, HEAD_DIM), ROW, split_axis=...  10.8 us
    all_to_all x1, waiting for transfers between devices, per_device(): owned = lax.all_to_all(send, ROW, split_axis=0, concat_axis=0, tiled=True)  9.06 us
    pallas_call x1, Pallas kernels, per_device(): pl.pallas_call(state_kernel, grid=(heads // n,), in_specs=[scalars, per_h...  7.33 us
  transfers between devices with their start and end apart: 19, of which 13 were waited for; matrix products, arithmetic and copies ran while one was open for 6% of the time, Pallas kernels for 15%

profile of v2, /device:TPU:0, one launch (start us, length us, event | category | flops | bytes accessed | tf_op | source)
XLA Modules:
  0.0 170.5 jit_solution(5463378359018287412)
XLA Ops:
  0.6 4.0 %collective-permute-start.1 = (bf16[64,2048]{1,0:T(8,128)(2,1)}, bf16[64,2048]{1,0:T(8,128)(2,1)S(1)}, u32[]{:S(2)}, u32[]{:S(2)}) collective-permute-start(bf16[64,2048]{1,0:T(8,128)(2,1)} %tok0_ref.1), channel_id=1, source_target_pairs={{0,2},{1,3},{2,0},{3,1},{4,6},{5,7},{6,4},{7,5},{8,10},{9,11},{10,... | collective-permute-start | bytes 786440 | tf_op jit(solution)/shard_map/ppermute | solution.py:367
  9.2 2.8 %collective-permute-done.1.tok2_ref = bf16[64,2048]{1,0:T(8,128)(2,1)S(1)} collective-permute-done((bf16[64,2048]{1,0:T(8,128)(2,1)}, bf16[64,2048]{1,0:T(8,128)(2,1)S(1)}, u32[]{:S(2)}, u32[]{:S(2)}) %collective-permute-start.1) | collective-permute-done | bytes 262176 | tf_op jit(solution)/shard_map/ppermute | solution.py:367
  12.0 5.6 %collective-permute-done.tok1_ref = bf16[64,2048]{1,0:T(8,128)(2,1)S(1)} collective-permute-done((bf16[64,2048]{1,0:T(8,128)(2,1)}, bf16[64,2048]{1,0:T(8,128)(2,1)S(1)}, u32[]{:S(2)}, u32[]{:S(2)}) %collective-permute-start) | collective-permute-done | bytes 262176 | tf_op jit(solution)/shard_map/ppermute | solution.py:367
  18.5 19.7 %transform.1 = (f32[256,512]{1,0:T(8,128)}, f32[256,512]{1,0:T(8,128)}, f32[256,512]{1,0:T(8,128)}, f32[4,4,128,128]{3,2,1,0:T(8,128)}, f32[4,4,128,256]{3,2,1,0...) custom-call(s32[2]{0:T(128)} %pad_add_fusion.at_ref, ...), custom_call_target="tpu_custom_call" | custom-call | tf_op jit(solution)/shard_map/transform/pallas_call | solution.py:439
  38.2 4.5 %all-to-all-start = ((f32[8,192,128]{2,1,0:T(8,128)}), f32[8,192,128]{2,1,0:T(8,128)S(1)}, u32[]{:S(2)}, u32[]{:S(2)}) async-start(f32[8,192,128]{2,1,0:T(8,128)} %get-tuple-element.23), calls=%async_computation | async-start | bytes 1572864 | tf_op jit(solution)/shard_map/all_to_all | solution.py:465
  46.8 9.1 %all-to-all-done.in_ref = f32[8,192,128]{2,1,0:T(8,128)S(1)} async-done(((f32[8,192,128]{2,1,0:T(8,128)}), f32[8,192,128]{2,1,0:T(8,128)S(1)}, u32[]{:S(2)}, u32[]{:S(2)}) %all-to-all-start) | async-done | bytes 786464 | tf_op jit(solution)/shard_map/all_to_all | solution.py:465
  57.1 2.8 %collective-permute-start.5 = (f32[192,128]{1,0:T(8,128)S(1)}, f32[192,128]{1,0:T(8,128)S(1)}, u32[]{:S(2)}, u32[]{:S(2)}) collective-permute-start(f32[192,128]{1,0:T(8,128)S(1)} %get-tuple-element.24.p0_ref), channel_id=1, source_target_pairs={{0,96},{32,64},{64,32},{96,0},{1,97},{33,65},{65,33},{97,1},{2,98}... | collective-permute-start | bytes 294920 | tf_op jit(solution)/shard_map/ppermute | solution.py:367
  60.7 3.2 %collective-permute-done.5.p3_ref = f32[192,128]{1,0:T(8,128)S(1)} collective-permute-done((f32[192,128]{1,0:T(8,128)S(1)}, f32[192,128]{1,0:T(8,128)S(1)}, u32[]{:S(2)}, u32[]{:S(2)}) %collective-permute-start.5) | collective-permute-done | bytes 98336 | tf_op jit(solution)/shard_map/ppermute | solution.py:367
  70.4 3.6 %all-to-all-start.1 = ((f32[8,64,128]{2,1,0:T(8,128)}), f32[8,64,128]{2,1,0:T(8,128)S(1)}, u32[]{:S(2)}, u32[]{:S(2)}) async-start(f32[8,64,128]{2,1,0:T(8,128)} %shard_map.105), calls=%async_computation.1 | async-start | bytes 524288 | tf_op jit(solution)/shard_map/all_to_all | solution.py:473
  74.1 2.7 %fusion = f32[256,512]{1,0:T(8,128)} fusion(bf16[512,2048]{1,0:T(8,128)(2,1)S(1)} %copy-done, bf16[64,2048]{1,0:T(8,128)(2,1)} %collective-permute-done.8, bf16[64,2048]{1,0:T(8,128)(2,1)} %collective-permute-done.7, bf16[64,2048]{1,0:T(8,128)(2,1)} %collective-permute-done.6, bf16[64,2048]{1,0:T(8,128)(2,1)} %param.17), kind=kOutput, calls=%fused_computation.1 | convolution fusion | flops 541065216 | bytes 3670016 | tf_op jit(solution)/shard_map/dot_general | solution.py:29
  76.8 4.5 %all-to-all-done.1 = f32[8,64,128]{2,1,0:T(8,128)S(1)} async-done(((f32[8,64,128]{2,1,0:T(8,128)}), f32[8,64,128]{2,1,0:T(8,128)S(1)}, u32[]{:S(2)}, u32[]{:S(2)}) %all-to-all-start.1) | async-done | bytes 262176 | tf_op jit(solution)/shard_map/all_to_all | solution.py:473
  82.0 7.3 %state.1 = (f32[4,4,128,128]{3,2,1,0:T(8,128)}, bf16[256,512]{1,0:T(8,128)(2,1)}, f32[256,512]{1,0:T(8,128)}, f32[4,4,128,128]{3,2,1,0:T(8,128)}, f32[4,128,128]{2,1,0:T(8,128)}) custom-call(s32[2]{0:T(128)} %pad_add_fusion.at_ref, f32[4,128,128]{2,1,0:T(8,128)} %bitcast.14, f32[4,4,256,128]{3,2,1,0:T(8,128)} %get-tuple-element.26.y_ref, ...), custom_call_target="tpu_custom_call" | custom-call | tf_op jit(solution)/shard_map/state/pallas_call | solution.py:478
  89.3 10.8 %all_to_all.25.c_ref = f32[8,64,128]{2,1,0:T(8,128)S(1)} all-to-all(f32[8,64,128]{2,1,0:T(8,128)} %bitcast.16), channel_id=1, replica_groups=mesh['ctx_0'=4,'ctx_1'=4,'ctx_2'=2,'head'=4] {'ctx_1','ctx_2'}, dimensions={0} | all-to-all | bytes 524288 | tf_op jit(solution)/shard_map/all_to_all | solution.py:499
  101.1 3.7 %collective-permute-start.11 = (f32[64,128]{1,0:T(8,128)S(1)}, f32[64,128]{1,0:T(8,128)S(1)}, u32[]{:S(2)}, u32[]{:S(2)}) collective-permute-start(f32[64,128]{1,0:T(8,128)S(1)} %shard_map.106.c0_ref), channel_id=1, source_target_pairs={{0,96},{32,64},{64,32},{96,0},{1,97},{33,65},{65,33},{97,1},{2,98}... | collective-permute-start | bytes 98312 | tf_op jit(solution)/shard_map/ppermute | solution.py:367
  106.7 3.5 %collective-permute-done.10.c2_ref = f32[64,128]{1,0:T(8,128)S(1)} collective-permute-done((f32[64,128]{1,0:T(8,128)S(1)}, f32[64,128]{1,0:T(8,128)S(1)}, u32[]{:S(2)}, u32[]{:S(2)}) %collective-permute-start.10) | collective-permute-done | bytes 32800 | tf_op jit(solution)/shard_map/ppermute | solution.py:367
  112.8 3.4 %all-to-all-start.4 = ((f32[8,64,128]{2,1,0:T(8,128)}), f32[8,64,128]{2,1,0:T(8,128)S(1)}, u32[]{:S(2)}, u32[]{:S(2)}) async-start(f32[8,64,128]{2,1,0:T(8,128)} %shard_map.107), calls=%async_computation.4 | async-start | bytes 524288 | tf_op jit(solution)/shard_map/all_to_all | solution.py:508
  116.2 2.7 %convolution_convert_fusion = bf16[256,2048]{1,0:T(8,128)(2,1)} fusion(bf16[256,512]{1,0:T(8,128)(2,1)} %get-tuple-element.29, bf16[512,2048]{1,0:T(8,128)(2,1)S(1)} %copy-done), kind=kOutput, calls=%fused_computation | convolution fusion | flops 537395200 | bytes 3407872 | tf_op jit(solution)/shard_map/dot_general | solution.py:29
  118.9 4.7 %all-to-all-done.4 = f32[8,64,128]{2,1,0:T(8,128)S(1)} async-done(((f32[8,64,128]{2,1,0:T(8,128)}), f32[8,64,128]{2,1,0:T(8,128)S(1)}, u32[]{:S(2)}, u32[]{:S(2)}) %all-to-all-start.4) | async-done | bytes 262176 | tf_op jit(solution)/shard_map/all_to_all | solution.py:508
  123.7 3.9 %all-to-all-start.2 = ((bf16[4,64,2048]{2,1,0:T(8,128)(2,1)}), bf16[4,64,2048]{2,1,0:T(8,128)(2,1)S(1)}, u32[]{:S(2)}, u32[]{:S(2)}) async-start(bf16[4,64,2048]{2,1,0:T(8,128)(2,1)} %bitcast.6), calls=%async_computation.2 | async-start | bytes 2097152 | tf_op jit(solution)/shard_map/all_to_all | solution.py:403
  127.6 21.9 %backward.1 = (bf16[64,2048]{1,0:T(8,128)(2,1)}, bf16[64,2048]{1,0:T(8,128)(2,1)}, bf16[64,2048]{1,0:T(8,128)(2,1)}, bf16[64,2048]{1,0:T(8,128)(2,1)}) custom-call(s32[2]{0:T(128)} %pad_add_fusion.at_ref, f32[4,128,128]{2,1,0:T(8,128)} %bitcast.13, f32[4,4,256,128]{3,2,1,0:T(8,128)} %get-tuple-element.26.y_ref, f32[4,4,128,128]{3,2,1,0:T(8,128)} %get-tuple-element.31.e_ref, ...), custom_call_target="tpu_custom_call" | custom-call | tf_op jit(solution)/shard_map/backward/pallas_call | solution.py:514
  151.5 2.7 %collective-permute-start.13 = (bf16[64,2048]{1,0:T(8,128)(2,1)}, bf16[64,2048]{1,0:T(8,128)(2,1)S(1)}, u32[]{:S(2)}, u32[]{:S(2)}) collective-permute-start(bf16[64,2048]{1,0:T(8,128)(2,1)} %get-tuple-element.42), channel_id=1, source_target_pairs={{0,2},{1,3},{2,0},{3,1},{4,6},{5,7},{6,4},{7,5},{8,10},{9,11},{10,... | collective-permute-start | bytes 786440 | tf_op jit(solution)/shard_map/ppermute | solution.py:537
  154.3 4.7 %collective-permute-done.12 = bf16[64,2048]{1,0:T(8,128)(2,1)S(1)} collective-permute-done((bf16[64,2048]{1,0:T(8,128)(2,1)}, bf16[64,2048]{1,0:T(8,128)(2,1)S(1)}, u32[]{:S(2)}, u32[]{:S(2)}) %collective-permute-start.12) | collective-permute-done | bytes 262176 | tf_op jit(solution)/shard_map/ppermute | solution.py:537
  159.0 6.3 %collective-permute-done.13 = bf16[64,2048]{1,0:T(8,128)(2,1)S(1)} collective-permute-done((bf16[64,2048]{1,0:T(8,128)(2,1)}, bf16[64,2048]{1,0:T(8,128)(2,1)S(1)}, u32[]{:S(2)}, u32[]{:S(2)}) %collective-permute-start.13) | collective-permute-done | bytes 262176 | tf_op jit(solution)/shard_map/ppermute | solution.py:537
  165.2 2.6 %collective-permute-done.14 = bf16[64,2048]{1,0:T(8,128)(2,1)S(1)} collective-permute-done((bf16[64,2048]{1,0:T(8,128)(2,1)}, bf16[64,2048]{1,0:T(8,128)(2,1)S(1)}, u32[]{:S(2)}, u32[]{:S(2)}) %collective-permute-start.14) | collective-permute-done | bytes 262176 | tf_op jit(solution)/shard_map/ppermute | solution.py:537
  (62 shorter events, 29.0 us)
Async XLA Ops:
  0.6 73.4 %copy-start = (bf16[512,2048]{1,0:T(8,128)(2,1)S(1)}, bf16[512,2048]{1,0:T(8,128)(2,1)}, u32[]{:S(2)}) copy-start(bf16[512,2048]{1,0:T(8,128)(2,1)} %param.15) | copy-start | bytes 6291460
  0.6 11.4 %collective-permute-start.1 = (bf16[64,2048]{1,0:T(8,128)(2,1)}, bf16[64,2048]{1,0:T(8,128)(2,1)S(1)}, u32[]{:S(2)}, u32[]{:S(2)}) collective-permute-start(bf16[64,2048]{1,0:T(8,128)(2,1)} %tok0_ref.1), channel_id=1, source_target_pairs={{0,2},{1,3},{2,0},{3,1},{4,6},{5,7},{6,4},{7,5},{8,10},{9,11},{10,... | collective-permute-start | bytes 786440 | tf_op jit(solution)/shard_map/ppermute | solution.py:367
  4.7 12.9 %collective-permute-start = (bf16[64,2048]{1,0:T(8,128)(2,1)}, bf16[64,2048]{1,0:T(8,128)(2,1)S(1)}, u32[]{:S(2)}, u32[]{:S(2)}) collective-permute-start(bf16[64,2048]{1,0:T(8,128)(2,1)} %tok0_ref.1), channel_id=1, source_target_pairs={{0,1},{1,0},{2,3},{3,2},{4,5},{5,4},{6,7},{7,6},{8,9},{9,8},{10,11... | collective-permute-start | bytes 786440 | tf_op jit(solution)/shard_map/ppermute | solution.py:367
  5.7 11.9 %collective-permute-start.2 = (bf16[64,2048]{1,0:T(8,128)(2,1)}, bf16[64,2048]{1,0:T(8,128)(2,1)S(1)}, u32[]{:S(2)}, u32[]{:S(2)}) collective-permute-start(bf16[64,2048]{1,0:T(8,128)(2,1)} %tok0_ref.1), channel_id=1, source_target_pairs={{0,3},{1,2},{2,1},{3,0},{4,7},{5,6},{6,5},{7,4},{8,11},{9,10},{10,... | collective-permute-start | bytes 786440 | tf_op jit(solution)/shard_map/ppermute | solution.py:367
  12.0 6.4 %copy-start.5 = (bf16[64,2048]{1,0:T(8,128)(2,1)}, bf16[64,2048]{1,0:T(8,128)(2,1)S(1)}, u32[]{:S(2)}) copy-start(bf16[64,2048]{1,0:T(8,128)(2,1)S(1)} %collective-permute-done.1.tok2_ref) | copy-start | bytes 786436
  38.2 30.3 %copy-start.1 = (s32[2]{0:T(128)S(1)}, s32[2]{0:T(128)}, u32[]{:S(2)}) copy-start(s32[2]{0:T(128)} %pad_add_fusion.at_ref) | copy-start | bytes 28
  38.2 17.6 %all-to-all-start = ((f32[8,192,128]{2,1,0:T(8,128)}), f32[8,192,128]{2,1,0:T(8,128)S(1)}, u32[]{:S(2)}, u32[]{:S(2)}) async-start(f32[8,192,128]{2,1,0:T(8,128)} %get-tuple-element.23), calls=%async_computation | async-start | bytes 1572864 | tf_op jit(solution)/shard_map/all_to_all | solution.py:465
  42.7 31.3 %collective-permute-start.7 = (bf16[64,2048]{1,0:T(8,128)(2,1)}, bf16[64,2048]{1,0:T(8,128)(2,1)}, u32[]{:S(2)}, u32[]{:S(2)}) collective-permute-start(bf16[64,2048]{1,0:T(8,128)(2,1)} %param.17), channel_id=1, source_target_pairs={{0,2},{1,3},{2,0},{3,1},{4,6},{5,7},{6,4},{7,5},{8,10},{9,11},{10,... | collective-permute-start | bytes 786440 | tf_op jit(solution)/shard_map/ppermute | solution.py:367
  45.1 28.9 %collective-permute-start.6 = (bf16[64,2048]{1,0:T(8,128)(2,1)}, bf16[64,2048]{1,0:T(8,128)(2,1)}, u32[]{:S(2)}, u32[]{:S(2)}) collective-permute-start(bf16[64,2048]{1,0:T(8,128)(2,1)} %param.17), channel_id=1, source_target_pairs={{0,1},{1,0},{2,3},{3,2},{4,5},{5,4},{6,7},{7,6},{8,9},{9,8},{10,11... | collective-permute-start | bytes 786440 | tf_op jit(solution)/shard_map/ppermute | solution.py:367
  46.2 27.9 %collective-permute-start.8 = (bf16[64,2048]{1,0:T(8,128)(2,1)}, bf16[64,2048]{1,0:T(8,128)(2,1)}, u32[]{:S(2)}, u32[]{:S(2)}) collective-permute-start(bf16[64,2048]{1,0:T(8,128)(2,1)} %param.17), channel_id=1, source_target_pairs={{0,3},{1,2},{2,1},{3,0},{4,7},{5,6},{6,5},{7,4},{8,11},{9,10},{10,... | collective-permute-start | bytes 786440 | tf_op jit(solution)/shard_map/ppermute | solution.py:367
  57.1 6.8 %collective-permute-start.5 = (f32[192,128]{1,0:T(8,128)S(1)}, f32[192,128]{1,0:T(8,128)S(1)}, u32[]{:S(2)}, u32[]{:S(2)}) collective-permute-start(f32[192,128]{1,0:T(8,128)S(1)} %get-tuple-element.24.p0_ref), channel_id=1, source_target_pairs={{0,96},{32,64},{64,32},{96,0},{1,97},{33,65},{65,33},{97,1},{2,98}... | collective-permute-start | bytes 294920 | tf_op jit(solution)/shard_map/ppermute | solution.py:367
  59.9 6.1 %collective-permute-start.4 = (f32[192,128]{1,0:T(8,128)S(1)}, f32[192,128]{1,0:T(8,128)S(1)}, u32[]{:S(2)}, u32[]{:S(2)}) collective-permute-start(f32[192,128]{1,0:T(8,128)S(1)} %get-tuple-element.24.p0_ref), channel_id=1, source_target_pairs={{0,64},{32,96},{64,0},{96,32},{1,65},{33,97},{65,1},{97,33},{2,66}... | collective-permute-start | bytes 294920 | tf_op jit(solution)/shard_map/ppermute | solution.py:367
  63.9 4.6 %collective-permute-start.3 = (f32[192,128]{1,0:T(8,128)S(1)}, f32[192,128]{1,0:T(8,128)S(1)}, u32[]{:S(2)}, u32[]{:S(2)}) collective-permute-start(f32[192,128]{1,0:T(8,128)S(1)} %get-tuple-element.24.p0_ref), channel_id=1, source_target_pairs={{0,32},{32,0},{64,96},{96,64},{1,33},{33,1},{65,97},{97,65},{2,34}... | collective-permute-start | bytes 294920 | tf_op jit(solution)/shard_map/ppermute | solution.py:367
  70.4 10.9 %all-to-all-start.1 = ((f32[8,64,128]{2,1,0:T(8,128)}), f32[8,64,128]{2,1,0:T(8,128)S(1)}, u32[]{:S(2)}, u32[]{:S(2)}) async-start(f32[8,64,128]{2,1,0:T(8,128)} %shard_map.105), calls=%async_computation.1 | async-start | bytes 524288 | tf_op jit(solution)/shard_map/all_to_all | solution.py:473
  82.0 28.2 %copy-start.2 = (s32[2]{0:T(128)S(1)}, s32[2]{0:T(128)}, u32[]{:S(2)}) copy-start(s32[2]{0:T(128)} %pad_add_fusion.at_ref) | copy-start | bytes 28
  101.1 5.6 %collective-permute-start.11 = (f32[64,128]{1,0:T(8,128)S(1)}, f32[64,128]{1,0:T(8,128)S(1)}, u32[]{:S(2)}, u32[]{:S(2)}) collective-permute-start(f32[64,128]{1,0:T(8,128)S(1)} %shard_map.106.c0_ref), channel_id=1, source_target_pairs={{0,96},{32,64},{64,32},{96,0},{1,97},{33,65},{65,33},{97,1},{2,98}... | collective-permute-start | bytes 98312 | tf_op jit(solution)/shard_map/ppermute | solution.py:367
  104.8 5.4 %collective-permute-start.10 = (f32[64,128]{1,0:T(8,128)S(1)}, f32[64,128]{1,0:T(8,128)S(1)}, u32[]{:S(2)}, u32[]{:S(2)}) collective-permute-start(f32[64,128]{1,0:T(8,128)S(1)} %shard_map.106.c0_ref), channel_id=1, source_target_pairs={{0,64},{32,96},{64,0},{96,32},{1,65},{33,97},{65,1},{97,33},{2,66}... | collective-permute-start | bytes 98312 | tf_op jit(solution)/shard_map/ppermute | solution.py:367
  104.8 5.4 %collective-permute-start.9 = (f32[64,128]{1,0:T(8,128)S(1)}, f32[64,128]{1,0:T(8,128)S(1)}, u32[]{:S(2)}, u32[]{:S(2)}) collective-permute-start(f32[64,128]{1,0:T(8,128)S(1)} %shard_map.106.c0_ref), channel_id=1, source_target_pairs={{0,32},{32,0},{64,96},{96,64},{1,33},{33,1},{65,97},{97,65},{2,34}... | collective-permute-start | bytes 98312 | tf_op jit(solution)/shard_map/ppermute | solution.py:367
  112.8 10.9 %all-to-all-start.4 = ((f32[8,64,128]{2,1,0:T(8,128)}), f32[8,64,128]{2,1,0:T(8,128)S(1)}, u32[]{:S(2)}, u32[]{:S(2)}) async-start(f32[8,64,128]{2,1,0:T(8,128)} %shard_map.107), calls=%async_computation.4 | async-start | bytes 524288 | tf_op jit(solution)/shard_map/all_to_all | solution.py:508
  123.7 3.9 %copy-start.3 = (f32[8,64,128]{2,1,0:T(8,128)}, f32[8,64,128]{2,1,0:T(8,128)S(1)}, u32[]{:S(2)}) copy-start(f32[8,64,128]{2,1,0:T(8,128)S(1)} %all-to-all-done.4) | copy-start | bytes 786436
  123.7 45.9 %all-to-all-start.2 = ((bf16[4,64,2048]{2,1,0:T(8,128)(2,1)}), bf16[4,64,2048]{2,1,0:T(8,128)(2,1)S(1)}, u32[]{:S(2)}, u32[]{:S(2)}) async-start(bf16[4,64,2048]{2,1,0:T(8,128)(2,1)} %bitcast.6), calls=%async_computation.2 | async-start | bytes 2097152 | tf_op jit(solution)/shard_map/all_to_all | solution.py:403
  149.4 9.5 %collective-permute-start.12 = (bf16[64,2048]{1,0:T(8,128)(2,1)}, bf16[64,2048]{1,0:T(8,128)(2,1)S(1)}, u32[]{:S(2)}, u32[]{:S(2)}) collective-permute-start(bf16[64,2048]{1,0:T(8,128)(2,1)} %get-tuple-element.41), channel_id=1, source_target_pairs={{0,1},{1,0},{2,3},{3,2},{4,5},{5,4},{6,7},{7,6},{8,9},{9,8},{10,11... | collective-permute-start | bytes 786440 | tf_op jit(solution)/shard_map/ppermute | solution.py:537
  151.5 13.7 %collective-permute-start.13 = (bf16[64,2048]{1,0:T(8,128)(2,1)}, bf16[64,2048]{1,0:T(8,128)(2,1)S(1)}, u32[]{:S(2)}, u32[]{:S(2)}) collective-permute-start(bf16[64,2048]{1,0:T(8,128)(2,1)} %get-tuple-element.42), channel_id=1, source_target_pairs={{0,2},{1,3},{2,0},{3,1},{4,6},{5,7},{6,4},{7,5},{8,10},{9,11},{10,... | collective-permute-start | bytes 786440 | tf_op jit(solution)/shard_map/ppermute | solution.py:537
  154.2 13.6 %collective-permute-start.14 = (bf16[64,2048]{1,0:T(8,128)(2,1)}, bf16[64,2048]{1,0:T(8,128)(2,1)S(1)}, u32[]{:S(2)}, u32[]{:S(2)}) collective-permute-start(bf16[64,2048]{1,0:T(8,128)(2,1)} %get-tuple-element.43), channel_id=1, source_target_pairs={{0,3},{1,2},{2,1},{3,0},{4,7},{5,6},{6,5},{7,4},{8,11},{9,10},{10,... | collective-permute-start | bytes 786440 | tf_op jit(solution)/shard_map/ppermute | solution.py:537
  (3 other events, 2.5 us)

commit v3 on v2

--- a/solution.py
+++ b/solution.py
@@ -16,7 +16,7 @@
 BF16 = jnp.bfloat16
 epsilon = 1e-06
 HEADS_FIRST = 2
-HEADS_STATE = 2
+HEADS_STATE = 4
 HEADS_BACK = 2
 MIB = 1 << 20
 LIMIT_FIRST = None
@@ -35,9 +35,13 @@
 
 
 def mm(a, b, ca=1, cb=0):
-    ah, al = split(a)
-    bh, bl = split(b)
-    if a.shape[ca] % 128:
+    return mm_halves(split(a), split(b), ca, cb)
+
+
+def mm_halves(a, b, ca=1, cb=0):
+    ah, al = a
+    bh, bl = b
+    if ah.shape[ca] % 128:
         return dot1(ah, bh, ca, cb) + (dot1(ah, bl, ca, cb) + dot1(al, bh, ca, cb))
     both = dot1(jnp.concatenate([ah, al], ca), jnp.concatenate([bh, bh], cb), ca, cb)
     return both + dot1(ah, bl, ca, cb)
@@ -56,7 +60,7 @@
 
 
 class Masks:
-    def __init__(self, rows_ref, cols_ref, groups):
+    def __init__(self, rows_ref, groups):
         self.pr = refl_pos(iota2(REFL, REFL, 0))
         self.pc = refl_pos(iota2(REFL, REFL, 1))
         self.eye = (self.pr == self.pc).astype(F32)
@@ -64,12 +68,11 @@
         tok = iota2(GROUP, REFL, 0)
         self.reach = (iota2(GROUP, REFL, 1) % GROUP) <= tok
         self.rows = rows_ref[...]
-        self.cols = cols_ref[...]
         self.groups = groups
 
     def of(self, g):
-        dc = self.cols[g * REFL : (g + 1) * REFL, :]
         dr = self.rows[g : g + 1, :]
+        dc = jnp.transpose(jnp.broadcast_to(dr, (REFL, REFL)))
         prev = self.rows[self.groups + g : self.groups + g + 1, :]
         last = self.rows[2 * self.groups + g : 2 * self.groups + g + 1, :]
         strict = jnp.logical_and(self.before, dc == dr)
@@ -100,7 +103,7 @@
 
 def transform_kernel(
     at_ref, tok0_ref, tok1_ref, tok2_ref, tok3_ref, wq_ref, wk1_ref, wk2_ref, wv1_ref, wv2_ref,
-    rows_ref, cols_ref,
+    rows_ref,
     q_ref, k1_ref, k2_ref, t_ref, x_ref, s_ref, qt_ref, ol_ref, y_ref, send_ref, tok_ref,
 ):
     at = at_ref[0]
@@ -120,7 +123,7 @@
     q_ref[...] = q
     k1_ref[...] = k1
     k2_ref[...] = k2
-    masks = Masks(rows_ref, cols_ref, groups)
+    masks = Masks(rows_ref, groups)
     per = [masks.of(g) for g in range(groups)]
     plain = (iota2(HEAD_DIM, HEAD_DIM, 0) == iota2(HEAD_DIM, HEAD_DIM, 1)).astype(F32)
     every = [(h, g) for h in heads_in(q_ref) for g in range(groups)]
@@ -219,13 +222,13 @@
 
 def backward_kernel(
     at_ref, dn_ref, y_ref, e_ref, n_ref, x_ref, s_ref, t_ref, q_ref, k1_ref, k2_ref, do_ref,
-    rows_ref, cols_ref, wq_ref, wk1_ref, wk2_ref, wv1_ref, wv2_ref,
+    rows_ref, wq_ref, wk1_ref, wk2_ref, wv1_ref, wv2_ref,
     out0_ref, out1_ref, out2_ref, out3_ref, acc_ref,
 ):
     at = at_ref[0]
     groups = y_ref.shape[1]
     heads = heads_in(q_ref)
-    masks = Masks(rows_ref, cols_ref, groups)
+    masks = Masks(rows_ref, groups)
     per = [masks.of(g) for g in range(groups)]
     after = {}
     grad_state = {h: dn_ref[h] for h in heads}
@@ -392,9 +395,7 @@
     twice = jnp.concatenate([here, here], axis=1)
     prev = jnp.broadcast_to(doc_of(starts - 1)[:, None], (groups, REFL))
     last = jnp.broadcast_to(doc_of(starts + GROUP - 1)[:, None], (groups, REFL))
-    rows_mark = jnp.concatenate([twice, prev, last, jnp.zeros_like(last)], axis=0)
-    cols_mark = jnp.broadcast_to(twice.reshape(groups * REFL, 1), (groups * REFL, HEAD_DIM))
-    return rows_mark, cols_mark
+    return jnp.concatenate([twice, prev, last, jnp.zeros_like(last)], axis=0)
 
 
 def sum_at_owner(value, axis):
@@ -420,7 +421,7 @@
     row_size = lax.axis_size(ROW)
     parts = row_size // heads
     cut = HEAD_DIM // parts
-    rows_mark, cols_mark = document_marks(lengths, lax.axis_index(CTX) * rows, rows)
+    rows_mark = document_marks(lengths, lax.axis_index(CTX) * rows, rows)
     at = jnp.stack([lax.axis_index("head"), lax.axis_index("ctx_0")]).astype(jnp.int32)
     scalars = pl.BlockSpec(memory_space=pltpu.SMEM)
 
@@ -441,7 +442,7 @@
         grid=(heads // n,),
         in_specs=[
             scalars, *[fixed(share, width)] * shards, *w_specs(n),
-            fixed(*rows_mark.shape), fixed(*cols_mark.shape),
+            fixed(*rows_mark.shape),
         ],
         out_specs=[
             lane_block(rows, n), lane_block(rows, n), lane_block(rows, n),
@@ -460,7 +461,7 @@
         scratch_shapes=[pltpu.VMEM((shards, share, width), BF16)],
         compiler_params=params(LIMIT_FIRST),
         name="transform",
-    )(at, *token_parts, *weights, rows_mark, cols_mark)
+    )(at, *token_parts, *weights, rows_mark)
 
     owned = lax.all_to_all(send, ROW, split_axis=0, concat_axis=0, tiled=True)
     prefix, plane = whole(row_chain_kernel, [owned.shape, owned.shape[1:]], owned)
@@ -474,7 +475,7 @@
     start = start.reshape(heads, HEAD_DIM, HEAD_DIM)
     grad_normed = dot1(jnp.concatenate(cotangent_parts, axis=0), w_out, 1, 1)
 
-    n = HEADS_STATE
+    n = min(HEADS_STATE, heads)
     states, normed, grad_mixed, ends, carried = pl.pallas_call(
         state_kernel,
         grid=(heads // n,),
@@ -501,6 +502,8 @@
     )
     (plane_back,) = whole(row_back_kernel, [(cut, HEAD_DIM)], owned, owned_back)
     back_planes = exchanged(plane_back, "ctx_0")
+    result_part = dot1(normed, w_out, 1, 0).astype(BF16)
+    back_planes, result_part = lax.optimization_barrier((back_planes, result_part))
     (row_grads,) = whole(
         row_grads_kernel, [(row_size, cut, HEAD_DIM)],
         at, *planes, *back_planes, owned, owned_back, scalar=True, scratch=plane_scratch,
@@ -508,7 +511,7 @@
     end_grad = lax.all_to_all(row_grads, ROW, split_axis=0, concat_axis=0, tiled=True)
     end_grad = end_grad.reshape(heads, HEAD_DIM, HEAD_DIM)
 
-    result = sum_at_owner(dot1(normed, w_out, 1, 0).astype(BF16), "head")
+    result = sum_at_owner(result_part, "head")
 
     n = HEADS_BACK
     summed = pl.pallas_call(
@@ -520,7 +523,7 @@
             per_head(n, groups, REFL, 2 * HEAD_DIM), per_head(n, groups, GROUP, REFL),
             per_head(n, groups, REFL, REFL), lane_block(rows, n), lane_block(rows, n),
             lane_block(rows, n), lane_block(rows, n),
-            fixed(*rows_mark.shape), fixed(*cols_mark.shape), *w_specs(n),
+            fixed(*rows_mark.shape), *w_specs(n),
         ],
         out_specs=[fixed(share, width)] * shards,
         out_shape=[jax.ShapeDtypeStruct((share, width), BF16)] * shards,
@@ -529,7 +532,7 @@
         name="backward",
     )(
         at, end_grad, steps, ends, states, x, scores, inverse, q, k1, k2, grad_mixed,
-        rows_mark, cols_mark, *weights,
+        rows_mark, *weights,
     )
     grad_tokens = summed[0].astype(F32)
     for rel in range(1, shards):

time: 171 us -> 169 us (0.988)
  blocking collectives: 10.8 us -> 21.5 us
  waiting for transfers between devices: 52.5 us -> 45.3 us
  starting transfers between devices: 37.7 us -> 33.9 us
  Pallas kernels: 55.5 us -> 53.7 us
    all_to_all x0 -> x1, blocking collectives: none -> 10.6 us  [per_device(): lax.all_to_all(row_grads, ROW, split_axis=0, concat_axis=0, tiled=True)]
    all_to_all x1 -> x0, waiting for transfers between devices: 4.75 us -> none  [per_device(): lax.all_to_all(row_grads, ROW, split_axis=0, concat_axis=0, tiled=True)]
    all_to_all x1 -> x0, starting transfers between devices: 3.41 us -> none  [per_device(): lax.all_to_all(row_grads, ROW, split_axis=0, concat_axis=0, tiled=True)]
    ppermute x12, waiting for transfers between devices: 20.7 us -> 17.9 us  [exchanged(): lax.ppermute(value, axis, [(j, j ^ rel) for j in range(count)])]
  transfers between devices with their start and end apart: 19 -> 18, of which waited for: 13 -> 11; matrix products, arithmetic and copies ran while one was open for 6% -> 6% of each run, Pallas kernels for 15% -> 15%
where the time goes in v3:
time: 169 us
  Pallas kernels  53.7 us (32%)
  waiting for transfers between devices  45.3 us (27%)
  starting transfers between devices  33.9 us (20%)
  blocking collectives  21.5 us (13%)
  matrix products  5.44 us (3%)
  other arithmetic  5.19 us (3%)
  local copies, waits for them, and re-layouts  3.18 us (2%)
    pallas_call x1, Pallas kernels, per_device(): pl.pallas_call(backward_kernel, grid=(heads // n,), in_specs=[scalars, pe...  22.1 us
    pallas_call x1, Pallas kernels, per_device(): pl.pallas_call(transform_kernel, grid=(heads // n,), in_specs=[scalars, *...  19.9 us
    ppermute x12, waiting for transfers between devices, exchanged(): lax.ppermute(value, axis, [(j, j ^ rel) for j in range(count)])  17.9 us
    ppermute x12, starting transfers between devices, exchanged(): lax.ppermute(value, axis, [(j, j ^ rel) for j in range(count)])  17.5 us
    ppermute x3, waiting for transfers between devices, per_device(): lax.ppermute(summed[rel], 'head', to_owner).astype(F32)  13.8 us
    all_to_all x1, blocking collectives, per_device(): lax.all_to_all(carried.reshape(row_size, cut, HEAD_DIM), ROW, split_axis=...  10.8 us
    all_to_all x1, blocking collectives, per_device(): lax.all_to_all(row_grads, ROW, split_axis=0, concat_axis=0, tiled=True)  10.6 us
    all_to_all x1, waiting for transfers between devices, per_device(): owned = lax.all_to_all(send, ROW, split_axis=0, concat_axis=0, tiled=True)  9.06 us
  transfers between devices with their start and end apart: 18, of which 11 were waited for; matrix products, arithmetic and copies ran while one was open for 6% of the time, Pallas kernels for 15%

profile of v3, /device:TPU:0, one launch (start us, length us, event | category | flops | bytes accessed | tf_op | source)
XLA Modules:
  0.0 168.9 jit_solution(4715259270704779343)
XLA Ops:
  0.6 4.0 %collective-permute-start.1 = (bf16[64,2048]{1,0:T(8,128)(2,1)}, bf16[64,2048]{1,0:T(8,128)(2,1)S(1)}, u32[]{:S(2)}, u32[]{:S(2)}) collective-permute-start(bf16[64,2048]{1,0:T(8,128)(2,1)} %tok0_ref.1), channel_id=1, source_target_pairs={{0,2},{1,3},{2,0},{3,1},{4,6},{5,7},{6,4},{7,5},{8,10},{9,11},{10,... | collective-permute-start | bytes 786440 | tf_op jit(solution)/shard_map/ppermute | solution.py:370
  9.2 2.8 %collective-permute-done.1.tok2_ref = bf16[64,2048]{1,0:T(8,128)(2,1)S(1)} collective-permute-done((bf16[64,2048]{1,0:T(8,128)(2,1)}, bf16[64,2048]{1,0:T(8,128)(2,1)S(1)}, u32[]{:S(2)}, u32[]{:S(2)}) %collective-permute-start.1) | collective-permute-done | bytes 262176 | tf_op jit(solution)/shard_map/ppermute | solution.py:370
  12.0 5.6 %collective-permute-done.tok1_ref = bf16[64,2048]{1,0:T(8,128)(2,1)S(1)} collective-permute-done((bf16[64,2048]{1,0:T(8,128)(2,1)}, bf16[64,2048]{1,0:T(8,128)(2,1)S(1)}, u32[]{:S(2)}, u32[]{:S(2)}) %collective-permute-start) | collective-permute-done | bytes 262176 | tf_op jit(solution)/shard_map/ppermute | solution.py:370
  19.0 19.9 %transform.1 = (f32[256,512]{1,0:T(8,128)}, f32[256,512]{1,0:T(8,128)}, f32[256,512]{1,0:T(8,128)}, f32[4,4,128,128]{3,2,1,0:T(8,128)}, f32[4,4,128,256]{3,2,1,0...) custom-call(s32[2]{0:T(128)} %pad_add_fusion.at_ref, ...), custom_call_target="tpu_custom_call" | custom-call | tf_op jit(solution)/shard_map/transform/pallas_call | solution.py:440
  38.9 4.5 %all-to-all-start = ((f32[8,192,128]{2,1,0:T(8,128)}), f32[8,192,128]{2,1,0:T(8,128)S(1)}, u32[]{:S(2)}, u32[]{:S(2)}) async-start(f32[8,192,128]{2,1,0:T(8,128)} %get-tuple-element.28), calls=%async_computation | async-start | bytes 1572864 | tf_op jit(solution)/shard_map/all_to_all | solution.py:466
  47.5 9.1 %all-to-all-done.in_ref = f32[8,192,128]{2,1,0:T(8,128)S(1)} async-done(((f32[8,192,128]{2,1,0:T(8,128)}), f32[8,192,128]{2,1,0:T(8,128)S(1)}, u32[]{:S(2)}, u32[]{:S(2)}) %all-to-all-start) | async-done | bytes 786464 | tf_op jit(solution)/shard_map/all_to_all | solution.py:466
  57.8 2.8 %collective-permute-start.5 = (f32[192,128]{1,0:T(8,128)S(1)}, f32[192,128]{1,0:T(8,128)S(1)}, u32[]{:S(2)}, u32[]{:S(2)}) collective-permute-start(f32[192,128]{1,0:T(8,128)S(1)} %get-tuple-element.29.p0_ref), channel_id=1, source_target_pairs={{0,96},{32,64},{64,32},{96,0},{1,97},{33,65},{65,33},{97,1},{2,98}... | collective-permute-start | bytes 294920 | tf_op jit(solution)/shard_map/ppermute | solution.py:370
  61.4 3.2 %collective-permute-done.5.p3_ref = f32[192,128]{1,0:T(8,128)S(1)} collective-permute-done((f32[192,128]{1,0:T(8,128)S(1)}, f32[192,128]{1,0:T(8,128)S(1)}, u32[]{:S(2)}, u32[]{:S(2)}) %collective-permute-start.5) | collective-permute-done | bytes 98336 | tf_op jit(solution)/shard_map/ppermute | solution.py:370
  64.6 2.1 %collective-permute-done.4.p2_ref = f32[192,128]{1,0:T(8,128)S(1)} collective-permute-done((f32[192,128]{1,0:T(8,128)S(1)}, f32[192,128]{1,0:T(8,128)S(1)}, u32[]{:S(2)}, u32[]{:S(2)}) %collective-permute-start.4) | collective-permute-done | bytes 98336 | tf_op jit(solution)/shard_map/ppermute | solution.py:370
  66.7 2.5 %collective-permute-done.3.p1_ref = f32[192,128]{1,0:T(8,128)S(1)} collective-permute-done((f32[192,128]{1,0:T(8,128)S(1)}, f32[192,128]{1,0:T(8,128)S(1)}, u32[]{:S(2)}, u32[]{:S(2)}) %collective-permute-start.3) | collective-permute-done | bytes 98336 | tf_op jit(solution)/shard_map/ppermute | solution.py:370
  71.1 3.6 %all-to-all-start.1 = ((f32[8,64,128]{2,1,0:T(8,128)}), f32[8,64,128]{2,1,0:T(8,128)S(1)}, u32[]{:S(2)}, u32[]{:S(2)}) async-start(f32[8,64,128]{2,1,0:T(8,128)} %shard_map.105), calls=%async_computation.1 | async-start | bytes 524288 | tf_op jit(solution)/shard_map/all_to_all | solution.py:474
  74.8 2.7 %fusion = f32[256,512]{1,0:T(8,128)} fusion(bf16[512,2048]{1,0:T(8,128)(2,1)S(1)} %copy-done, bf16[64,2048]{1,0:T(8,128)(2,1)} %collective-permute-done.8, bf16[64,2048]{1,0:T(8,128)(2,1)} %collective-permute-done.7, bf16[64,2048]{1,0:T(8,128)(2,1)} %collective-permute-done.6, bf16[64,2048]{1,0:T(8,128)(2,1)} %param.17), kind=kOutput, calls=%fused_computation.1 | convolution fusion | flops 541065216 | bytes 3670016 | tf_op jit(solution)/shard_map/dot_general | solution.py:29
  77.5 4.5 %all-to-all-done.1 = f32[8,64,128]{2,1,0:T(8,128)S(1)} async-done(((f32[8,64,128]{2,1,0:T(8,128)}), f32[8,64,128]{2,1,0:T(8,128)S(1)}, u32[]{:S(2)}, u32[]{:S(2)}) %all-to-all-start.1) | async-done | bytes 262176 | tf_op jit(solution)/shard_map/all_to_all | solution.py:474
  82.7 5.8 %state.1 = (f32[4,4,128,128]{3,2,1,0:T(8,128)}, bf16[256,512]{1,0:T(8,128)(2,1)}, f32[256,512]{1,0:T(8,128)}, f32[4,4,128,128]{3,2,1,0:T(8,128)}, f32[4,128,128]{2,1,0:T(8,128)}) custom-call(s32[2]{0:T(128)} %pad_add_fusion.at_ref, f32[4,128,128]{2,1,0:T(8,128)} %bitcast.13, f32[4,4,256,128]{3,2,1,0:T(8,128)} %get-tuple-element.31.y_ref, ...), custom_call_target="tpu_custom_call" | custom-call | tf_op jit(solution)/shard_map/state/pallas_call | solution.py:479
  88.6 10.8 %all_to_all.25.c_ref = f32[8,64,128]{2,1,0:T(8,128)S(1)} all-to-all(f32[8,64,128]{2,1,0:T(8,128)} %bitcast.15), channel_id=1, replica_groups=mesh['ctx_0'=4,'ctx_1'=4,'ctx_2'=2,'head'=4] {'ctx_1','ctx_2'}, dimensions={0} | all-to-all | bytes 524288 | tf_op jit(solution)/shard_map/all_to_all | solution.py:500
  100.3 3.7 %collective-permute-start.11 = (f32[64,128]{1,0:T(8,128)S(1)}, f32[64,128]{1,0:T(8,128)S(1)}, u32[]{:S(2)}, u32[]{:S(2)}) collective-permute-start(f32[64,128]{1,0:T(8,128)S(1)} %shard_map.106.c0_ref), channel_id=1, source_target_pairs={{0,96},{32,64},{64,32},{96,0},{1,97},{33,65},{65,33},{97,1},{2,98}... | collective-permute-start | bytes 98312 | tf_op jit(solution)/shard_map/ppermute | solution.py:370
  105.0 2.7 %convolution_convert_fusion = bf16[256,2048]{1,0:T(8,128)(2,1)} fusion(bf16[256,512]{1,0:T(8,128)(2,1)} %get-tuple-element.35, bf16[512,2048]{1,0:T(8,128)(2,1)S(1)} %copy-done), kind=kOutput, calls=%fused_computation | convolution fusion | flops 537395200 | bytes 3407872 | tf_op jit(solution)/shard_map/dot_general | solution.py:29
  111.3 10.6 %all_to_all.26 = f32[8,64,128]{2,1,0:T(8,128)} all-to-all(f32[8,64,128]{2,1,0:T(8,128)S(1)} %shard_map.107), channel_id=1, replica_groups=mesh['ctx_0'=4,'ctx_1'=4,'ctx_2'=2,'head'=4] {'ctx_1','ctx_2'}, dimensions={0} | all-to-all | bytes 524288 | tf_op jit(solution)/shard_map/all_to_all | solution.py:511
  121.9 3.5 %all-to-all-start.3 = ((bf16[4,64,2048]{2,1,0:T(8,128)(2,1)}), bf16[4,64,2048]{2,1,0:T(8,128)(2,1)S(1)}, u32[]{:S(2)}, u32[]{:S(2)}) async-start(bf16[4,64,2048]{2,1,0:T(8,128)(2,1)} %bitcast.11), calls=%async_computation.3 | async-start | bytes 2097152 | tf_op jit(solution)/shard_map/all_to_all | solution.py:404
  125.5 22.1 %backward.1 = (bf16[64,2048]{1,0:T(8,128)(2,1)}, bf16[64,2048]{1,0:T(8,128)(2,1)}, bf16[64,2048]{1,0:T(8,128)(2,1)}, bf16[64,2048]{1,0:T(8,128)(2,1)}) custom-call(s32[2]{0:T(128)} %pad_add_fusion.at_ref, f32[4,128,128]{2,1,0:T(8,128)} %bitcast.12, f32[4,4,256,128]{3,2,1,0:T(8,128)} %get-tuple-element.31.y_ref, f32[4,4,128,128]{3,2,1,0:T(8,128)} %get-tuple-element.41.e_ref, ...), custom_call_target="tpu_custom_call" | custom-call | tf_op jit(solution)/shard_map/backward/pallas_call | solution.py:517
  149.6 2.7 %collective-permute-start.13 = (bf16[64,2048]{1,0:T(8,128)(2,1)}, bf16[64,2048]{1,0:T(8,128)(2,1)S(1)}, u32[]{:S(2)}, u32[]{:S(2)}) collective-permute-start(bf16[64,2048]{1,0:T(8,128)(2,1)} %get-tuple-element.52), channel_id=1, source_target_pairs={{0,2},{1,3},{2,0},{3,1},{4,6},{5,7},{6,4},{7,5},{8,10},{9,11},{10,... | collective-permute-start | bytes 786440 | tf_op jit(solution)/shard_map/ppermute | solution.py:540
  152.4 4.7 %collective-permute-done.12 = bf16[64,2048]{1,0:T(8,128)(2,1)S(1)} collective-permute-done((bf16[64,2048]{1,0:T(8,128)(2,1)}, bf16[64,2048]{1,0:T(8,128)(2,1)S(1)}, u32[]{:S(2)}, u32[]{:S(2)}) %collective-permute-start.12) | collective-permute-done | bytes 262176 | tf_op jit(solution)/shard_map/ppermute | solution.py:540
  157.1 6.5 %collective-permute-done.13 = bf16[64,2048]{1,0:T(8,128)(2,1)S(1)} collective-permute-done((bf16[64,2048]{1,0:T(8,128)(2,1)}, bf16[64,2048]{1,0:T(8,128)(2,1)S(1)}, u32[]{:S(2)}, u32[]{:S(2)}) %collective-permute-start.13) | collective-permute-done | bytes 262176 | tf_op jit(solution)/shard_map/ppermute | solution.py:540
  163.6 2.6 %collective-permute-done.14 = bf16[64,2048]{1,0:T(8,128)(2,1)S(1)} collective-permute-done((bf16[64,2048]{1,0:T(8,128)(2,1)}, bf16[64,2048]{1,0:T(8,128)(2,1)S(1)}, u32[]{:S(2)}, u32[]{:S(2)}) %collective-permute-start.14) | collective-permute-done | bytes 262176 | tf_op jit(solution)/shard_map/ppermute | solution.py:540
  (57 shorter events, 25.0 us)
Async XLA Ops:
  0.6 74.1 %copy-start = (bf16[512,2048]{1,0:T(8,128)(2,1)S(1)}, bf16[512,2048]{1,0:T(8,128)(2,1)}, u32[]{:S(2)}) copy-start(bf16[512,2048]{1,0:T(8,128)(2,1)} %param.15) | copy-start | bytes 6291460
  0.6 11.4 %collective-permute-start.1 = (bf16[64,2048]{1,0:T(8,128)(2,1)}, bf16[64,2048]{1,0:T(8,128)(2,1)S(1)}, u32[]{:S(2)}, u32[]{:S(2)}) collective-permute-start(bf16[64,2048]{1,0:T(8,128)(2,1)} %tok0_ref.1), channel_id=1, source_target_pairs={{0,2},{1,3},{2,0},{3,1},{4,6},{5,7},{6,4},{7,5},{8,10},{9,11},{10,... | collective-permute-start | bytes 786440 | tf_op jit(solution)/shard_map/ppermute | solution.py:370
  4.7 12.9 %collective-permute-start = (bf16[64,2048]{1,0:T(8,128)(2,1)}, bf16[64,2048]{1,0:T(8,128)(2,1)S(1)}, u32[]{:S(2)}, u32[]{:S(2)}) collective-permute-start(bf16[64,2048]{1,0:T(8,128)(2,1)} %tok0_ref.1), channel_id=1, source_target_pairs={{0,1},{1,0},{2,3},{3,2},{4,5},{5,4},{6,7},{7,6},{8,9},{9,8},{10,11... | collective-permute-start | bytes 786440 | tf_op jit(solution)/shard_map/ppermute | solution.py:370
  5.7 11.9 %collective-permute-start.2 = (bf16[64,2048]{1,0:T(8,128)(2,1)}, bf16[64,2048]{1,0:T(8,128)(2,1)S(1)}, u32[]{:S(2)}, u32[]{:S(2)}) collective-permute-start(bf16[64,2048]{1,0:T(8,128)(2,1)} %tok0_ref.1), channel_id=1, source_target_pairs={{0,3},{1,2},{2,1},{3,0},{4,7},{5,6},{6,5},{7,4},{8,11},{9,10},{10,... | collective-permute-start | bytes 786440 | tf_op jit(solution)/shard_map/ppermute | solution.py:370
  12.0 5.6 %copy-start.4 = (bf16[64,2048]{1,0:T(8,128)(2,1)}, bf16[64,2048]{1,0:T(8,128)(2,1)S(1)}, u32[]{:S(2)}) copy-start(bf16[64,2048]{1,0:T(8,128)(2,1)S(1)} %collective-permute-done.1.tok2_ref) | copy-start | bytes 786436
  17.6 0.7 copy-start.5
  18.3 0.7 copy-start.6
  38.9 30.3 %copy-start.1 = (s32[2]{0:T(128)S(1)}, s32[2]{0:T(128)}, u32[]{:S(2)}) copy-start(s32[2]{0:T(128)} %pad_add_fusion.at_ref) | copy-start | bytes 28
  38.9 17.6 %all-to-all-start = ((f32[8,192,128]{2,1,0:T(8,128)}), f32[8,192,128]{2,1,0:T(8,128)S(1)}, u32[]{:S(2)}, u32[]{:S(2)}) async-start(f32[8,192,128]{2,1,0:T(8,128)} %get-tuple-element.28), calls=%async_computation | async-start | bytes 1572864 | tf_op jit(solution)/shard_map/all_to_all | solution.py:466
  43.4 31.3 %collective-permute-start.7 = (bf16[64,2048]{1,0:T(8,128)(2,1)}, bf16[64,2048]{1,0:T(8,128)(2,1)}, u32[]{:S(2)}, u32[]{:S(2)}) collective-permute-start(bf16[64,2048]{1,0:T(8,128)(2,1)} %param.17), channel_id=1, source_target_pairs={{0,2},{1,3},{2,0},{3,1},{4,6},{5,7},{6,4},{7,5},{8,10},{9,11},{10,... | collective-permute-start | bytes 786440 | tf_op jit(solution)/shard_map/ppermute | solution.py:370
  45.2 29.6 %collective-permute-start.6 = (bf16[64,2048]{1,0:T(8,128)(2,1)}, bf16[64,2048]{1,0:T(8,128)(2,1)}, u32[]{:S(2)}, u32[]{:S(2)}) collective-permute-start(bf16[64,2048]{1,0:T(8,128)(2,1)} %param.17), channel_id=1, source_target_pairs={{0,1},{1,0},{2,3},{3,2},{4,5},{5,4},{6,7},{7,6},{8,9},{9,8},{10,11... | collective-permute-start | bytes 786440 | tf_op jit(solution)/shard_map/ppermute | solution.py:370
  46.2 28.6 %collective-permute-start.8 = (bf16[64,2048]{1,0:T(8,128)(2,1)}, bf16[64,2048]{1,0:T(8,128)(2,1)}, u32[]{:S(2)}, u32[]{:S(2)}) collective-permute-start(bf16[64,2048]{1,0:T(8,128)(2,1)} %param.17), channel_id=1, source_target_pairs={{0,3},{1,2},{2,1},{3,0},{4,7},{5,6},{6,5},{7,4},{8,11},{9,10},{10,... | collective-permute-start | bytes 786440 | tf_op jit(solution)/shard_map/ppermute | solution.py:370
  57.8 6.8 %collective-permute-start.5 = (f32[192,128]{1,0:T(8,128)S(1)}, f32[192,128]{1,0:T(8,128)S(1)}, u32[]{:S(2)}, u32[]{:S(2)}) collective-permute-start(f32[192,128]{1,0:T(8,128)S(1)} %get-tuple-element.29.p0_ref), channel_id=1, source_target_pairs={{0,96},{32,64},{64,32},{96,0},{1,97},{33,65},{65,33},{97,1},{2,98}... | collective-permute-start | bytes 294920 | tf_op jit(solution)/shard_map/ppermute | solution.py:370
  60.6 6.1 %collective-permute-start.4 = (f32[192,128]{1,0:T(8,128)S(1)}, f32[192,128]{1,0:T(8,128)S(1)}, u32[]{:S(2)}, u32[]{:S(2)}) collective-permute-start(f32[192,128]{1,0:T(8,128)S(1)} %get-tuple-element.29.p0_ref), channel_id=1, source_target_pairs={{0,64},{32,96},{64,0},{96,32},{1,65},{33,97},{65,1},{97,33},{2,66}... | collective-permute-start | bytes 294920 | tf_op jit(solution)/shard_map/ppermute | solution.py:370
  64.6 4.6 %collective-permute-start.3 = (f32[192,128]{1,0:T(8,128)S(1)}, f32[192,128]{1,0:T(8,128)S(1)}, u32[]{:S(2)}, u32[]{:S(2)}) collective-permute-start(f32[192,128]{1,0:T(8,128)S(1)} %get-tuple-element.29.p0_ref), channel_id=1, source_target_pairs={{0,32},{32,0},{64,96},{96,64},{1,33},{33,1},{65,97},{97,65},{2,34}... | collective-permute-start | bytes 294920 | tf_op jit(solution)/shard_map/ppermute | solution.py:370
  71.1 10.9 %all-to-all-start.1 = ((f32[8,64,128]{2,1,0:T(8,128)}), f32[8,64,128]{2,1,0:T(8,128)S(1)}, u32[]{:S(2)}, u32[]{:S(2)}) async-start(f32[8,64,128]{2,1,0:T(8,128)} %shard_map.105), calls=%async_computation.1 | async-start | bytes 524288 | tf_op jit(solution)/shard_map/all_to_all | solution.py:474
  99.4 10.1 %copy-start.2 = (s32[2]{0:T(128)S(1)}, s32[2]{0:T(128)}, u32[]{:S(2)}) copy-start(s32[2]{0:T(128)} %pad_add_fusion.at_ref) | copy-start | bytes 28
  100.3 7.4 %collective-permute-start.11 = (f32[64,128]{1,0:T(8,128)S(1)}, f32[64,128]{1,0:T(8,128)S(1)}, u32[]{:S(2)}, u32[]{:S(2)}) collective-permute-start(f32[64,128]{1,0:T(8,128)S(1)} %shard_map.106.c0_ref), channel_id=1, source_target_pairs={{0,96},{32,64},{64,32},{96,0},{1,97},{33,65},{65,33},{97,1},{2,98}... | collective-permute-start | bytes 98312 | tf_op jit(solution)/shard_map/ppermute | solution.py:370
  104.1 5.4 %collective-permute-start.10 = (f32[64,128]{1,0:T(8,128)S(1)}, f32[64,128]{1,0:T(8,128)S(1)}, u32[]{:S(2)}, u32[]{:S(2)}) collective-permute-start(f32[64,128]{1,0:T(8,128)S(1)} %shard_map.106.c0_ref), channel_id=1, source_target_pairs={{0,64},{32,96},{64,0},{96,32},{1,65},{33,97},{65,1},{97,33},{2,66}... | collective-permute-start | bytes 98312 | tf_op jit(solution)/shard_map/ppermute | solution.py:370
  104.1 5.4 %collective-permute-start.9 = (f32[64,128]{1,0:T(8,128)S(1)}, f32[64,128]{1,0:T(8,128)S(1)}, u32[]{:S(2)}, u32[]{:S(2)}) collective-permute-start(f32[64,128]{1,0:T(8,128)S(1)} %shard_map.106.c0_ref), channel_id=1, source_target_pairs={{0,32},{32,0},{64,96},{96,64},{1,33},{33,1},{65,97},{97,65},{2,34}... | collective-permute-start | bytes 98312 | tf_op jit(solution)/shard_map/ppermute | solution.py:370
  121.9 46.0 %all-to-all-start.3 = ((bf16[4,64,2048]{2,1,0:T(8,128)(2,1)}), bf16[4,64,2048]{2,1,0:T(8,128)(2,1)S(1)}, u32[]{:S(2)}, u32[]{:S(2)}) async-start(bf16[4,64,2048]{2,1,0:T(8,128)(2,1)} %bitcast.11), calls=%async_computation.3 | async-start | bytes 2097152 | tf_op jit(solution)/shard_map/all_to_all | solution.py:404
  147.6 9.5 %collective-permute-start.12 = (bf16[64,2048]{1,0:T(8,128)(2,1)}, bf16[64,2048]{1,0:T(8,128)(2,1)S(1)}, u32[]{:S(2)}, u32[]{:S(2)}) collective-permute-start(bf16[64,2048]{1,0:T(8,128)(2,1)} %get-tuple-element.51), channel_id=1, source_target_pairs={{0,1},{1,0},{2,3},{3,2},{4,5},{5,4},{6,7},{7,6},{8,9},{9,8},{10,11... | collective-permute-start | bytes 786440 | tf_op jit(solution)/shard_map/ppermute | solution.py:540
  149.6 14.0 %collective-permute-start.13 = (bf16[64,2048]{1,0:T(8,128)(2,1)}, bf16[64,2048]{1,0:T(8,128)(2,1)S(1)}, u32[]{:S(2)}, u32[]{:S(2)}) collective-permute-start(bf16[64,2048]{1,0:T(8,128)(2,1)} %get-tuple-element.52), channel_id=1, source_target_pairs={{0,2},{1,3},{2,0},{3,1},{4,6},{5,7},{6,4},{7,5},{8,10},{9,11},{10,... | collective-permute-start | bytes 786440 | tf_op jit(solution)/shard_map/ppermute | solution.py:540
  152.3 13.9 %collective-permute-start.14 = (bf16[64,2048]{1,0:T(8,128)(2,1)}, bf16[64,2048]{1,0:T(8,128)(2,1)S(1)}, u32[]{:S(2)}, u32[]{:S(2)}) collective-permute-start(bf16[64,2048]{1,0:T(8,128)(2,1)} %get-tuple-element.53), channel_id=1, source_target_pairs={{0,3},{1,2},{2,1},{3,0},{4,7},{5,6},{6,5},{7,4},{8,11},{9,10},{10,... | collective-permute-start | bytes 786440 | tf_op jit(solution)/shard_map/ppermute | solution.py:540
  (1 other events, 0.7 us)
